TPU v7x, 32 devices: a whole 2x2x4 slice. The times are simulated.
32 devices in a mesh: grp: 4 (over x, core), blk: 8 (over z, y).
Axes of the slice: x: 2, y: 2, z: 4, core: 2. Of those that a mesh axis runs over, the one named last changes fastest.
Arguments:
- residual: float32 [3, 16, 128, 512], P(None, 'blk', None, 'grp'), may hold values from -8 to 8
- face_mask: int32 [3, 16, 128, 512], P(None, 'blk', None, 'grp'), may hold values 0 or 1
- conductivity: float32 [4, 16, 128, 512], P('grp', 'blk'), may hold values from 0.5 to 4
- stencil: float32 [4, 27, 3, 3], replicated, may hold values from -1.5 to 1.5, as said below
Outputs:
- correction: float32 [3, 16, 128, 512], P(None, 'blk', None, 'grp')
Inputs may be any that keep to these rules, and one draw needn't show every extreme that they name: In each space's stencil the diagonal of the block at offset 0 exceeds the sum of magnitudes of all other entries of its row.
All inputs are finite; a program needn't handle non-finite values. No bound on the sum of `face_mask` on one device may be relied on, other than what follows from the above.
Results may differ from a plain program's by a relative error of at most 0.0001.
Values sent between devices are 32-bit elements; how exact they have to be, the bound alone decides.
A program may use at most 192 MiB of HBM per device.

v0:
```python
import jax
import jax.numpy as jnp
from jax import lax
from jax.sharding import PartitionSpec as P

OMEGA = 0.8


def extended(block, sides, width):
    for axis, dim in sides:
        count = lax.axis_size(axis)
        forward = [(i, i + 1) for i in range(count - 1)]
        backward = [(target, source) for source, target in forward]
        low = lax.ppermute(
            lax.slice_in_dim(block, block.shape[dim] - width, None, axis=dim), axis, forward
        )
        high = lax.ppermute(lax.slice_in_dim(block, 0, width, axis=dim), axis, backward)
        block = jnp.concatenate([low, block, high], axis=dim)
    return block


def place_of(shift_x, shift_y, shift_z):
    return 9 * (shift_x + 1) + 3 * (shift_y + 1) + (shift_z + 1)


def blank_tables():
    return [
        [[[0.0, 0.0, 0.0] for row_one in range(3)] for place in range(27)] for space in range(4)
    ]


def restriction_tables():
    forward = blank_tables()
    centre = place_of(0, 0, 0)
    for comp in range(3):
        forward[0][centre][comp][comp] = 1.0
        others = [axis_one for axis_one in range(3) if axis_one != comp]
        for first_off in (0, -1):
            for second_off in (0, -1):
                vector = [0, 0, 0]
                vector[others[0]] = first_off
                vector[others[1]] = second_off
                forward[1][place_of(*vector)][comp][comp] += 0.25
        along_p = (comp + 1) % 3
        along_q = (comp + 2) % 3
        forward[2][centre][comp][along_q] += 1.0
        forward[2][centre][comp][along_p] -= 1.0
        vector = [0, 0, 0]
        vector[along_p] = -1
        forward[2][place_of(*vector)][comp][along_q] -= 1.0
        vector = [0, 0, 0]
        vector[along_q] = -1
        forward[2][place_of(*vector)][comp][along_p] += 1.0
    for comp in range(3):
        for shift_x in (-1, 0, 1):
            for shift_y in (-1, 0, 1):
                for shift_z in (-1, 0, 1):
                    source = list(forward[2][place_of(shift_x, shift_y, shift_z)][comp])
                    if abs(source[0]) + abs(source[1]) + abs(source[2]) == 0:
                        continue
                    vector = [shift_x, shift_y, shift_z]
                    vector[comp] += 1
                    for column in range(3):
                        forward[3][place_of(shift_x, shift_y, shift_z)][comp][column] += (
                            0.5 * source[column]
                        )
                        forward[3][place_of(*vector)][comp][column] += 0.5 * source[column]
    backward = blank_tables()
    for space in range(4):
        for shift_x in (-1, 0, 1):
            for shift_y in (-1, 0, 1):
                for shift_z in (-1, 0, 1):
                    for row_one in range(3):
                        for column in range(3):
                            backward[space][place_of(-shift_x, -shift_y, -shift_z)][row_one][
                                column
                            ] = forward[space][place_of(shift_x, shift_y, shift_z)][column][row_one]
    return (forward, backward)


def pad_rest(field):
    return jnp.pad(field, ((0, 0), (0, 0), (1, 1), (1, 1)))


def dense_apply(table, padded):
    rows_x = padded.shape[1] - 2
    rows_y = padded.shape[2] - 2
    rows_z = padded.shape[3] - 2
    total = jnp.zeros((3, rows_x, rows_y, rows_z), jnp.float32)
    for shift_x in (-1, 0, 1):
        for shift_y in (-1, 0, 1):
            for shift_z in (-1, 0, 1):
                piece = padded[
                    :,
                    1 + shift_x : 1 + shift_x + rows_x,
                    1 + shift_y : 1 + shift_y + rows_y,
                    1 + shift_z : 1 + shift_z + rows_z,
                ]
                block = table[place_of(shift_x, shift_y, shift_z)]
                total = total + (block[:, :, None, None, None] * piece[None]).sum(1)
    return total


def sparse_apply(table, padded):
    rows_x = padded.shape[1] - 2
    rows_y = padded.shape[2] - 2
    rows_z = padded.shape[3] - 2
    outputs = [jnp.zeros((rows_x, rows_y, rows_z), jnp.float32) for comp in range(3)]
    for shift_x in (-1, 0, 1):
        for shift_y in (-1, 0, 1):
            for shift_z in (-1, 0, 1):
                block = table[place_of(shift_x, shift_y, shift_z)]
                for row_one in range(3):
                    for column in range(3):
                        weight = block[row_one][column]
                        if weight == 0.0:
                            continue
                        piece = padded[
                            column,
                            1 + shift_x : 1 + shift_x + rows_x,
                            1 + shift_y : 1 + shift_y + rows_y,
                            1 + shift_z : 1 + shift_z + rows_z,
                        ]
                        outputs[row_one] = outputs[row_one] + weight * piece
    return jnp.stack(outputs, 0)


def pick_apply(tables, group, padded):
    branches = [lambda field, table=tables[space]: sparse_apply(table, field) for space in range(4)]
    return lax.switch(group, branches, padded)


def local(residual, face_mask, conductivity, stencil):
    mask_float = face_mask.astype(jnp.float32)
    masked = residual * mask_float
    forward, backward = restriction_tables()
    group = lax.axis_index("grp")
    operator = stencil[group]
    centre = jnp.diagonal(operator[13])
    coeff = conductivity[0][None]
    scale = OMEGA / (coeff * centre[:, None, None, None])
    whole = lax.all_gather(masked, "grp", axis=3, tiled=True)
    padded = extended(whole, (("blk", 1),), 1)
    restricted = pick_apply(forward, group, pad_rest(padded))
    first = restricted * scale
    first_padded = extended(first, (("blk", 1),), 1)
    applied = coeff * dense_apply(operator, pad_rest(first_padded))
    second = first + (restricted - applied) * scale
    second_padded = extended(second, (("blk", 1),), 1)
    prolonged = pick_apply(backward, group, pad_rest(second_padded))
    owned = lax.psum_scatter(prolonged, "grp", scatter_dimension=3, tiled=True)
    return owned * mask_float


def solution(mesh):
    return jax.shard_map(
        local,
        mesh=mesh,
        in_specs=(
            P(None, "blk", None, "grp"),
            P(None, "blk", None, "grp"),
            P("grp", "blk", None, None),
            P(),
        ),
        out_specs=P(None, "blk", None, "grp"),
        check_vma=False,
    )
```

profile of v0, /device:TPU:9, one launch (start us, length us, event | category | flops | bytes accessed | tf_op | source)
XLA Modules:
  0.0 287.5 jit_solution(4037326965826820311)
XLA Ops:
  6.5 0.0 all-gather.2.cloned.1.call-start
  6.5 1.9 convert_multiply_fusion.1
  8.4 0.0 all-gather.2.cloned.1.call-update
  8.5 0.0 copy-start.21
  8.5 0.0 reduce-scatter.2.cloned.1.call-start
  8.5 21.8 %all-gather.2.cloned.1.call-done = f32[3,2,128,512]{3,2,1,0:T(8,128)} async-done(((f32[3,2,128,128]{3,2,1,0:T(8,128)}), f32[3,2,128,512]{3,2,1,0:T(8,128)}) %all-gather.2.cloned.1.call-update) | async-done | bytes 1572880 | tf_op jit(solution)/shard_map/all_gather | solution.py:142
  30.3 2.8 fusion.35
  33.1 3.1 %collective-permute-start = (f32[3,1,128,512]{3,2,1,0:T(8,128)}, f32[3,1,128,512]{3,2,1,0:T(8,128)S(1)}, u32[]{:S(2)}, u32[]{:S(2)}) collective-permute-start(f32[3,1,128,512]{3,2,1,0:T(8,128)} %get-tuple-element.96), channel_id=1, source_target_pairs={{0,1},{1,2},{2,3},{3,4},{4,5},{5,6},{6,7},{8,9},{9,10},{10,11},{11... | collective-permute-start | bytes 2359304 | tf_op jit(solution)/shard_map/ppermute | solution.py:14
  36.2 3.1 %collective-permute-start.1 = (f32[3,1,128,512]{3,2,1,0:T(8,128)}, f32[3,1,128,512]{3,2,1,0:T(8,128)S(1)}, u32[]{:S(2)}, u32[]{:S(2)}) collective-permute-start(f32[3,1,128,512]{3,2,1,0:T(8,128)} %get-tuple-element.97), channel_id=1, source_target_pairs={{1,0},{2,1},{3,2},{4,3},{5,4},{6,5},{7,6},{9,8},{10,9},{11,10},{12... | collective-permute-start | bytes 2359304 | tf_op jit(solution)/shard_map/ppermute | solution.py:17
  39.3 0.0 copy-done.21
  39.3 0.4 fusion.8
  39.7 0.7 gather_fusion
  40.4 29.7 %collective-permute-done = f32[3,1,128,512]{3,2,1,0:T(8,128)S(1)} collective-permute-done((f32[3,1,128,512]{3,2,1,0:T(8,128)}, f32[3,1,128,512]{3,2,1,0:T(8,128)S(1)}, u32[]{:S(2)}, u32[]{:S(2)}) %collective-permute-start) | collective-permute-done | bytes 786464 | tf_op jit(solution)/shard_map/ppermute | solution.py:14
  70.0 2.4 collective-permute-done.1
  72.5 0.0 copy-done.1
  72.5 3.7 %select_maximum_fusion.4 = f32[3,4,130,514]{3,2,1,0:T(8,128)} fusion(f32[3,1,128,512]{3,2,1,0:T(8,128)S(1)} %collective-permute-done.1, f32[3,2,128,512]{3,2,1,0:T(8,128)S(1)} %copy-done.1, f32[3,1,128,512]{3,2,1,0:T(8,128)S(1)} %collective-permute-done), kind=kLoop, calls=%fused_computation.60 | loop fusion | flops 12027600 | bytes 6353088 | tf_op jit(solution)/shard_map/concatenate | solution.py:18
  76.1 4.9 %conditional.2 = (f32[3,2,128,512]{3,2,1,0:T(8,128)S(1)}) conditional(s32[]{:T(128)} %clamp.4, f32[3,4,130,514]{3,2,1,0:T(8,128)} %select_maximum_fusion.4, f32[3,4,130,514]{3,2,1,0:T(8,128)} %select_maximum_fusion.4, f32[3,4,130,514]{3,2,1,0:T(8,128)} %select_maximum_fusion.4, ...), branch_computations={%region_0.1_spmd, %region_1.2_spmd, %region_2.3_spmd, %region_3.4_... | conditional | flops 6422528 | bytes 16777224 | solution.py:130
  76.1 4.7 %add_multiply_fusion.2 = (f32[1,2,128,512]{3,2,1,0:T(8,128)S(1)}, f32[1,2,128,512]{3,2,1,0:T(8,128)S(1)}, f32[1,2,128,512]{3,2,1,0:T(8,128)S(1)}) fusion(f32[3,4,130,514]{3,2,1,0:T(8,128)} %param.1), kind=kLoop, calls=%fused_computation.4 | loop fusion | flops 1572864 | bytes 7864320 | tf_op jit(solution)/shard_map/cond/branch_1_fun/add | solution.py:124
  80.8 0.2 pad_maximum_fusion
  81.0 1.4 fusion.3
  82.5 1.3 fusion.34
  83.7 1.9 collective-permute-start.2
  85.6 4.5 %collective-permute-start.3 = (f32[3,1,128,512]{3,2,1,0:T(8,128)}, f32[3,1,128,512]{3,2,1,0:T(8,128)}, u32[]{:S(2)}, u32[]{:S(2)}) collective-permute-start(f32[3,1,128,512]{3,2,1,0:T(8,128)} %get-tuple-element.95), channel_id=1, source_target_pairs={{1,0},{2,1},{3,2},{4,3},{5,4},{6,5},{7,6},{9,8},{10,9},{11,10},{12... | collective-permute-start | bytes 2359304 | tf_op jit(solution)/shard_map/ppermute | solution.py:17
  90.2 0.6 fusion.7
  90.7 0.4 multiply_reduce_fusion.13
  91.2 27.5 %collective-permute-done.2 = f32[3,1,128,512]{3,2,1,0:T(8,128)} collective-permute-done((f32[3,1,128,512]{3,2,1,0:T(8,128)}, f32[3,1,128,512]{3,2,1,0:T(8,128)}, u32[]{:S(2)}, u32[]{:S(2)}) %collective-permute-start.2) | collective-permute-done | bytes 786464 | tf_op jit(solution)/shard_map/ppermute | solution.py:14
  118.7 2.7 collective-permute-done.3
  121.4 3.5 %select_maximum_fusion.2 = f32[3,4,130,514]{3,2,1,0:T(8,128)S(1)} fusion(f32[3,1,128,512]{3,2,1,0:T(8,128)} %collective-permute-done.3, f32[3,2,128,512]{3,2,1,0:T(8,128)S(1)} %fusion.3, f32[3,1,128,512]{3,2,1,0:T(8,128)} %collective-permute-done.2), kind=kLoop, calls=%fused_computation.58 | loop fusion | flops 12027600 | bytes 6353088 | tf_op jit(solution)/shard_map/concatenate | solution.py:18
  124.9 11.0 %fusion.31 = (f32[3,2,128,512]{3,2,1,0:T(8,128)}, f32[3,2,128,512]{3,2,1,0:T(8,128)}, f32[3,2,128,512]{3,2,1,0:T(8,128)}, f32[3,2,128,512]{3,2,1,0:T(8,128)}, f3...) fusion(f32[3,4,130,514]{3,2,1,0:T(8,128)S(1)} %select_maximum_f, ...), kind=kLoop, calls=%fused_computation.127 | loop fusion | bytes 59768832 | tf_op jit(solution)/shard_map/slice | solution.py:93
  135.9 0.0 copy-start.19
  135.9 1.7 fusion.32
  137.7 2.8 multiply_reduce_fusion.19
  140.5 2.4 multiply_reduce_fusion.17
  142.9 2.4 multiply_reduce_fusion.15
  145.4 2.4 multiply_reduce_fusion.12
  147.8 0.0 copy-done.11
  147.8 2.4 multiply_reduce_fusion.10
  150.2 2.4 multiply_reduce_fusion.8
  152.7 0.0 copy-done.8
  152.7 2.4 multiply_reduce_fusion.6
  155.1 1.7 pad_maximum_fusion.7
  156.8 2.5 multiply_reduce_fusion.4
  159.3 2.5 multiply_reduce_fusion.21
  161.8 2.4 multiply_reduce_fusion.3
  164.2 0.0 copy-done.4
  164.2 2.4 multiply_reduce_fusion.1
  166.6 2.4 multiply_reduce_fusion
  169.0 12.4 %multiply_reduce_fusion.23 = (f32[3,2,128,512]{3,2,1,0:T(8,128)}, f32[3,2,128,512]{3,2,1,0:T(8,128)}) fusion(f32[3,2,128,512]{3,2,1,0:T(8,128)S(1)} %get-tuple-element.87, f32[3,3]{1,0:T(4,128)S(1)} %get-tuple-element.47, f32[3,2,128,512]{3,2,1,0:T(8,128)S(1)} %get-tuple-element.88, f32[3,3]{1,0:T(4,128)S(1)} %get-tuple-element.41), kind=kLoop, calls=%fused_computation.52 | loop fusion | flops 3932160 | bytes 6291528 | tf_op jit(solution)/shard_map/reduce_sum | solution.py:100
  181.4 0.0 copy-done
  181.4 14.3 %multiply_add_fusion.8 = f32[3,2,128,512]{3,2,1,0:T(8,128)S(1)} fusion(f32[3,2,128,512]{3,2,1,0:T(8,128)S(1)} %get-tuple-element.124, f32[3,2,128,512]{3,2,1,0:T(8,128)} %get-tuple-element.98, f32[3,2,128,512]{3,2,1,0:T(8,128)} %get-tuple-element.106, f32[3,2,128,512]{3,2,1,0:T(8,128)} %get-tuple-element.107, f32[3,2,128,512]{3,2,1,0:T(8,128)} %get-tuple-element.108, ...), kind=kLoop, calls=%fused_computation.67 | loop fusion | flops 12976128 | bytes 46137356 | tf_op jit(solution)/shard_map/add | solution.py:148
  195.7 0.2 fusion.33
  195.9 1.9 collective-permute-start.4
  197.8 4.3 %collective-permute-start.5 = (f32[3,1,128,512]{3,2,1,0:T(8,128)S(1)}, f32[3,1,128,512]{3,2,1,0:T(8,128)S(1)}, u32[]{:S(2)}, u32[]{:S(2)}) collective-permute-start(f32[3,1,128,512]{3,2,1,0:T(8,128)S(1)} %get-tuple-element.91), channel_id=1, source_target_pairs={{1,0},{2,1},{3,2},{4,3},{5,4},{6,5},{7,6},{9,8},{10,9},{11,10},{12... | collective-permute-start | bytes 2359304 | tf_op jit(solution)/shard_map/ppermute | solution.py:17
  202.1 29.3 %collective-permute-done.4 = f32[3,1,128,512]{3,2,1,0:T(8,128)S(1)} collective-permute-done((f32[3,1,128,512]{3,2,1,0:T(8,128)S(1)}, f32[3,1,128,512]{3,2,1,0:T(8,128)S(1)}, u32[]{:S(2)}, u32[]{:S(2)}) %collective-permute-start.4) | collective-permute-done | bytes 786464 | tf_op jit(solution)/shard_map/ppermute | solution.py:14
  231.5 3.6 %collective-permute-done.5 = f32[3,1,128,512]{3,2,1,0:T(8,128)S(1)} collective-permute-done((f32[3,1,128,512]{3,2,1,0:T(8,128)S(1)}, f32[3,1,128,512]{3,2,1,0:T(8,128)S(1)}, u32[]{:S(2)}, u32[]{:S(2)}) %collective-permute-start.5) | collective-permute-done | bytes 786464 | tf_op jit(solution)/shard_map/ppermute | solution.py:17
  235.0 3.7 %select_maximum_fusion = f32[3,4,130,514]{3,2,1,0:T(8,128)} fusion(f32[3,1,128,512]{3,2,1,0:T(8,128)S(1)} %collective-permute-done.5, f32[3,2,128,512]{3,2,1,0:T(8,128)S(1)} %multiply_add_fusion.8, f32[3,1,128,512]{3,2,1,0:T(8,128)S(1)} %collective-permute-done.4), kind=kLoop, calls=%fused_computation.56 | loop fusion | flops 12027600 | bytes 6353088 | tf_op jit(solution)/shard_map/concatenate | solution.py:18
  238.7 6.3 %conditional.3 = (f32[3,2,128,512]{3,2,1,0:T(8,128)S(1)}) conditional(s32[]{:T(128)} %clamp.4, f32[3,4,130,514]{3,2,1,0:T(8,128)} %select_maximum_fusion, f32[3,4,130,514]{3,2,1,0:T(8,128)} %select_maximum_fusion, f32[3,4,130,514]{3,2,1,0:T(8,128)} %select_maximum_fusion, ...), branch_computations={%region_31.32_spmd, %region_32.33_spmd, %region_33.34_spmd, %regio... | conditional | flops 6684672 | bytes 16252936 | solution.py:130
  238.7 6.1 %add_multiply_fusion.5 = (f32[1,2,128,512]{3,2,1,0:T(8,128)S(1)}, f32[1,2,128,512]{3,2,1,0:T(8,128)S(1)}, f32[1,2,128,512]{3,2,1,0:T(8,128)S(1)}) fusion(f32[3,4,130,514]{3,2,1,0:T(8,128)} %param.5), kind=kLoop, calls=%fused_computation.16 | loop fusion | flops 1572864 | bytes 7864320 | tf_op jit(solution)/shard_map/cond/branch_1_fun/add | solution.py:124
  244.8 0.2 pad_maximum_fusion.3
  245.0 0.0 copy-start.20
  245.0 1.1 copy-done.2
  246.1 0.0 reduce-scatter.2.cloned.1.call-update
  246.2 32.5 %reduce-scatter.2.cloned.1.call-done = f32[3,2,128,128]{3,2,1,0:T(8,128)} async-done(((f32[3,2,128,512]{3,2,1,0:T(8,128)}), f32[3,2,128,128]{3,2,1,0:T(8,128)}) %reduce-scatter.2.cloned.1.call-update) | async-done | bytes 393232 | tf_op jit(solution)/shard_map/reduce_scatter | solution.py:151
  278.7 1.8 convert_multiply_fusion
  (35 shorter events, 0.1 us)
Async XLA Ops:
  6.5 23.8 %all-gather.2.cloned.1.call-start = ((), (), s32[]{:S(2)}) async-start(), calls=%async_computation.1 | async-start | bytes 1966080 | tf_op jit(solution)/shard_map/all_gather | solution.py:142
  8.5 30.9 %copy-start.21 = (f32[4,27,3,3]{1,0,3,2:T(4,128)S(1)}, f32[4,27,3,3]{1,0,3,2:T(4,128)}, u32[]{:S(2)}) copy-start(f32[4,27,3,3]{1,0,3,2:T(4,128)} %param.15) | copy-start | bytes 11668
  8.5 270.2 %reduce-scatter.2.cloned.1.call-start = ((), (), s32[]{:S(2)}) async-start(), calls=%async_computation.2 | async-start | bytes 1966080 | tf_op jit(solution)/shard_map/reduce_scatter | solution.py:151
  30.3 42.2 %copy-start.1 = (f32[3,2,128,512]{3,2,1,0:T(8,128)S(1)}, f32[3,2,128,512]{3,2,1,0:T(8,128)}, u32[]{:S(2)}) copy-start(f32[3,2,128,512]{3,2,1,0:T(8,128)} %all-gather.2.cloned.1.call-done) | copy-start | bytes 4718596
  33.1 36.9 %collective-permute-start = (f32[3,1,128,512]{3,2,1,0:T(8,128)}, f32[3,1,128,512]{3,2,1,0:T(8,128)S(1)}, u32[]{:S(2)}, u32[]{:S(2)}) collective-permute-start(f32[3,1,128,512]{3,2,1,0:T(8,128)} %get-tuple-element.96), channel_id=1, source_target_pairs={{0,1},{1,2},{2,3},{3,4},{4,5},{5,6},{6,7},{8,9},{9,10},{10,11},{11... | collective-permute-start | bytes 2359304 | tf_op jit(solution)/shard_map/ppermute | solution.py:14
  36.2 36.2 %collective-permute-start.1 = (f32[3,1,128,512]{3,2,1,0:T(8,128)}, f32[3,1,128,512]{3,2,1,0:T(8,128)S(1)}, u32[]{:S(2)}, u32[]{:S(2)}) collective-permute-start(f32[3,1,128,512]{3,2,1,0:T(8,128)} %get-tuple-element.97), channel_id=1, source_target_pairs={{1,0},{2,1},{3,2},{4,3},{5,4},{6,5},{7,6},{9,8},{10,9},{11,10},{12... | collective-permute-start | bytes 2359304 | tf_op jit(solution)/shard_map/ppermute | solution.py:17
  83.7 35.0 %collective-permute-start.2 = (f32[3,1,128,512]{3,2,1,0:T(8,128)}, f32[3,1,128,512]{3,2,1,0:T(8,128)}, u32[]{:S(2)}, u32[]{:S(2)}) collective-permute-start(f32[3,1,128,512]{3,2,1,0:T(8,128)} %get-tuple-element.94), channel_id=1, source_target_pairs={{0,1},{1,2},{2,3},{3,4},{4,5},{5,6},{6,7},{8,9},{9,10},{10,11},{11... | collective-permute-start | bytes 2359304 | tf_op jit(solution)/shard_map/ppermute | solution.py:14
  85.6 35.7 %collective-permute-start.3 = (f32[3,1,128,512]{3,2,1,0:T(8,128)}, f32[3,1,128,512]{3,2,1,0:T(8,128)}, u32[]{:S(2)}, u32[]{:S(2)}) collective-permute-start(f32[3,1,128,512]{3,2,1,0:T(8,128)} %get-tuple-element.95), channel_id=1, source_target_pairs={{1,0},{2,1},{3,2},{4,3},{5,4},{6,5},{7,6},{9,8},{10,9},{11,10},{12... | collective-permute-start | bytes 2359304 | tf_op jit(solution)/shard_map/ppermute | solution.py:17
  135.9 1.8 copy-start.19
  137.6 2.8 copy-start.17
  137.7 2.8 copy-start.18
  140.5 2.4 copy-start.15
  140.5 2.4 copy-start.16
  142.9 2.5 copy-start.13
  142.9 2.5 copy-start.14
  145.4 2.4 copy-start.11
  145.4 2.4 copy-start.12
  147.8 2.4 copy-start.9
  147.8 2.4 copy-start.10
  150.2 2.4 copy-start.7
  150.2 2.4 copy-start.8
  159.3 2.5 copy-start.5
  159.3 2.5 copy-start.6
  161.8 2.4 copy-start.3
  161.8 2.4 copy-start.4
  169.0 12.4 %copy-start = (f32[3,2,128,512]{3,2,1,0:T(8,128)S(1)}, f32[3,2,128,512]{3,2,1,0:T(8,128)}, u32[]{:S(2)}) copy-start(f32[3,2,128,512]{3,2,1,0:T(8,128)} %get-tuple-element.120) | copy-start | bytes 4718596
  195.9 35.5 %collective-permute-start.4 = (f32[3,1,128,512]{3,2,1,0:T(8,128)S(1)}, f32[3,1,128,512]{3,2,1,0:T(8,128)S(1)}, u32[]{:S(2)}, u32[]{:S(2)}) collective-permute-start(f32[3,1,128,512]{3,2,1,0:T(8,128)S(1)} %get-tuple-element.90), channel_id=1, source_target_pairs={{0,1},{1,2},{2,3},{3,4},{4,5},{5,6},{6,7},{8,9},{9,10},{10,11},{11... | collective-permute-start | bytes 2359304 | tf_op jit(solution)/shard_map/ppermute | solution.py:14
  197.8 37.2 %collective-permute-start.5 = (f32[3,1,128,512]{3,2,1,0:T(8,128)S(1)}, f32[3,1,128,512]{3,2,1,0:T(8,128)S(1)}, u32[]{:S(2)}, u32[]{:S(2)}) collective-permute-start(f32[3,1,128,512]{3,2,1,0:T(8,128)S(1)} %get-tuple-element.91), channel_id=1, source_target_pairs={{1,0},{2,1},{3,2},{4,3},{5,4},{6,5},{7,6},{9,8},{10,9},{11,10},{12... | collective-permute-start | bytes 2359304 | tf_op jit(solution)/shard_map/ppermute | solution.py:17
  245.0 1.2 copy-start.2
  245.0 33.7 %copy-start.20 = (s32[3,2,128,128]{3,2,1,0:T(8,128)S(1)}, s32[3,2,128,128]{3,2,1,0:T(8,128)}, u32[]{:S(2)}) copy-start(s32[3,2,128,128]{3,2,1,0:T(8,128)} %param.13) | copy-start | bytes 1179652
Sparse Core Ops, SparseCore 0:
  8.9 21.3 all-gather.1
  246.3 32.3 reduce-scatter.1
where the time goes:
time: 292 us; the launch traced here: 287 us
  waiting for transfers between devices  150 us (51%)
  other arithmetic  85.4 us (29%)
  local copies, waits for them, and re-layouts  19.8 us (7%)
  starting transfers between devices  18.8 us (6%)
  between operations  13.9 us (5%)
    ppermute x3, waiting for transfers between devices, extended(): lax.ppermute(lax.slice_in_dim(block, block.shape[dim] - width, None, axis...  86.5 us
    reduce_sum x14, other arithmetic, dense_apply(): total = total + (block[:, :, None, None, None] * piece[None]).sum(1)  42.3 us
    reduce_scatter x1, waiting for transfers between devices, local(): owned = lax.psum_scatter(prolonged, 'grp', scatter_dimension=3, tiled=True)  32.5 us
    all_gather x1, waiting for transfers between devices, local(): whole = lax.all_gather(masked, 'grp', axis=3, tiled=True)  21.8 us
    add x1, other arithmetic, local(): second = first + (restricted - applied) * scale  14.3 us
    slice x2, local copies, waits for them, and re-layouts, dense_apply(): padded[:, 1 + shift_x:1 + shift_x + rows_x, 1 + shift_y:1 + shift_y + row...  12.7 us
    concatenate x4, other arithmetic, extended(): block = jnp.concatenate([low, block, high], axis=dim)  12.5 us
    ppermute x3, starting transfers between devices, extended(): lax.ppermute(lax.slice_in_dim(block, 0, width, axis=dim), axis, backward)  11.9 us
  transfers between devices with their start and end apart: 8, of which 8 were waited for; matrix products, arithmetic and copies ran while one was open for 1% of the time, Pallas kernels for 0%

commit v1 on v0

v1 whole, which is shorter than its diff:
```python
import jax
import jax.numpy as jnp
from jax import lax
from jax.experimental import pallas as pl
from jax.experimental.pallas import tpu as pltpu
from jax.sharding import PartitionSpec as P

OMEGA = 0.8
PAD = 8


def place_of(shift_x, shift_y, shift_z):
    return 9 * (shift_x + 1) + 3 * (shift_y + 1) + (shift_z + 1)


def blank_tables():
    return [
        [[[0.0, 0.0, 0.0] for row_one in range(3)] for place in range(27)] for space in range(4)
    ]


def restriction_tables():
    forward = blank_tables()
    centre = place_of(0, 0, 0)
    for comp in range(3):
        forward[0][centre][comp][comp] = 1.0
        others = [axis_one for axis_one in range(3) if axis_one != comp]
        for first_off in (0, -1):
            for second_off in (0, -1):
                vector = [0, 0, 0]
                vector[others[0]] = first_off
                vector[others[1]] = second_off
                forward[1][place_of(*vector)][comp][comp] += 0.25
        along_p = (comp + 1) % 3
        along_q = (comp + 2) % 3
        forward[2][centre][comp][along_q] += 1.0
        forward[2][centre][comp][along_p] -= 1.0
        vector = [0, 0, 0]
        vector[along_p] = -1
        forward[2][place_of(*vector)][comp][along_q] -= 1.0
        vector = [0, 0, 0]
        vector[along_q] = -1
        forward[2][place_of(*vector)][comp][along_p] += 1.0
    for comp in range(3):
        for shift_x in (-1, 0, 1):
            for shift_y in (-1, 0, 1):
                for shift_z in (-1, 0, 1):
                    source = list(forward[2][place_of(shift_x, shift_y, shift_z)][comp])
                    if abs(source[0]) + abs(source[1]) + abs(source[2]) == 0:
                        continue
                    vector = [shift_x, shift_y, shift_z]
                    vector[comp] += 1
                    for column in range(3):
                        forward[3][place_of(shift_x, shift_y, shift_z)][comp][column] += (
                            0.5 * source[column]
                        )
                        forward[3][place_of(*vector)][comp][column] += 0.5 * source[column]
    backward = blank_tables()
    for space in range(4):
        for shift_x in (-1, 0, 1):
            for shift_y in (-1, 0, 1):
                for shift_z in (-1, 0, 1):
                    for row_one in range(3):
                        for column in range(3):
                            backward[space][place_of(-shift_x, -shift_y, -shift_z)][row_one][
                                column
                            ] = forward[space][place_of(shift_x, shift_y, shift_z)][column][row_one]
    return (forward, backward)


def terms_of(table):
    rows = [[] for comp in range(3)]
    for dx in (-1, 0, 1):
        for dy in (-1, 0, 1):
            for dz in (-1, 0, 1):
                for row in range(3):
                    for column in range(3):
                        weight = table[place_of(dx, dy, dz)][row][column]
                        if weight != 0.0:
                            rows[row].append((dx, dy, dz, column, weight))
    return rows


def weighted(terms, load):
    groups = {}
    for dx, dy, dz, column, weight in terms:
        piece = load(dx, dy, dz, column)
        held = groups.get(abs(weight))
        if held is None:
            groups[abs(weight)] = piece if weight > 0 else -piece
        else:
            groups[abs(weight)] = held + piece if weight > 0 else held - piece
    total = None
    for size, held in groups.items():
        held = held if size == 1.0 else held * size
        total = held if total is None else total + held
    return total


def ring(own, beside, step, lane):
    width = own.shape[-1]
    turn = 1 if step < 0 else width - 1
    edge = 0 if step < 0 else width - 1
    own_turned = pltpu.roll(own, turn, own.ndim - 1)
    beside_turned = pltpu.roll(beside, turn, own.ndim - 1)
    at_edge = lane == edge
    return (
        jnp.where(at_edge, beside_turned, own_turned),
        jnp.where(at_edge, own_turned, beside_turned),
    )


def compute(weights, inverse, m, mh, c, ch, mz, mhz, f, rs, inv, sec, b, edges, layers, tall):
    first_block, last_block, first_lanes, last_lanes = edges
    forward, backward = restriction_tables()
    rows = tall - 2 * PAD
    chunk = 16
    width = m.shape[-1]
    lane = lax.broadcasted_iota(jnp.int32, (chunk, width), 1)
    zeros = jnp.zeros((PAD, width), jnp.float32)
    count = rows // chunk

    def at(index, shift=0):
        return pl.ds(index * chunk + (PAD + shift), chunk)

    for side in (0, 1):
        edge = pl.ds(side * (rows + PAD), PAD)
        for layer in range(layers + 4):
            for comp in range(3):
                m[layer, comp, edge, :] = zeros
                mh[layer, comp, edge, :] = zeros
                for dz in (0, 1):
                    mz[dz, layer, comp, edge, :] = zeros
                    mhz[dz, layer, comp, edge, :] = zeros
        for comp in range(3):
            for layer in range(layers + 2):
                for dz in range(3):
                    f[dz, comp, layer, edge, :] = zeros
            for layer in range(layers):
                sec[comp, layer, edge, :] = zeros

    @pl.loop(0, (layers + 4) * 3)
    def _(plane):
        layer, comp = plane // 3, plane % 3

        @pl.loop(0, count)
        def _(i):
            own, beside = m[layer, comp, at(i), :], mh[layer, comp, at(i), :]
            for dz in (0, 1):
                one, other = ring(own, beside, 2 * dz - 1, lane)
                mz[dz, layer, comp, at(i), :] = one
                mhz[dz, layer, comp, at(i), :] = other

    for space in range(4):
        table = terms_of(forward[space])
        base = space * 243

        @pl.loop(0, layers + 2)
        def _(layer):
            off = jnp.logical_or(
                jnp.logical_and(first_block, layer == 0),
                jnp.logical_and(last_block, layer == layers + 1),
            )
            off_left = jnp.logical_or(off, first_lanes)
            off_right = jnp.logical_or(off, last_lanes)

            @pl.loop(0, count)
            def _(i):
                flat = pl.ds(i * chunk, chunk)
                scale = OMEGA / c[space, layer, flat, :]
                scale_h = OMEGA / ch[space, layer, flat, :]
                inv[layer, flat, :] = scale
                for comp in range(3):
                    def own(dx, dy, dz, column):
                        place = m if dz == 0 else mz.at[(dz + 1) // 2]
                        return place[layer + 1 + dx, column, at(i, dy), :]

                    def beside(dx, dy, dz, column):
                        place = mh if dz == 0 else mhz.at[(dz + 1) // 2]
                        return place[layer + 1 + dx, column, at(i, dy), :]

                    centre = inverse[space * 3 + comp]
                    restricted = weighted(table[comp], own)
                    rs[layer, comp, flat, :] = restricted
                    value = jnp.where(off, 0.0, restricted * (scale * centre))
                    value_h = weighted(table[comp], beside) * (scale_h * centre)
                    gone = jnp.where(lane == 0, off_right.astype(jnp.int32), off_left.astype(jnp.int32))
                    value_h = jnp.where(gone != 0, 0.0, value_h)
                    f[1, comp, layer, at(i), :] = value
                    f[0, comp, layer, at(i), :] = ring(value, value_h, -1, lane)[0]
                    f[2, comp, layer, at(i), :] = ring(value, value_h, 1, lane)[0]

        @pl.loop(0, count)
        def _(i):
            flat = pl.ds(i * chunk, chunk)
            total = [[None] * 3 for layer in range(layers)]
            for dy in (-1, 0, 1):
                for dz in (-1, 0, 1):
                    for column in range(3):
                        planes = [f[dz + 1, column, layer, at(i, dy), :] for layer in range(layers + 2)]
                        for dx in (-1, 0, 1):
                            for comp in range(3):
                                weight = weights[base + place_of(dx, dy, dz) * 9 + comp * 3 + column]
                                for layer in range(layers):
                                    piece = planes[layer + 1 + dx] * weight
                                    held = total[layer][comp]
                                    total[layer][comp] = piece if held is None else held + piece
            for layer in range(layers):
                scale = inv[layer + 1, flat, :]
                coeff = c[space, layer + 1, flat, :]
                for comp in range(3):
                    left = rs[layer + 1, comp, flat, :] - coeff * total[layer][comp]
                    value = f[1, comp, layer + 1, at(i), :]
                    sec[comp, layer, at(i), :] = value + left * (scale * inverse[space * 3 + comp])

        table = terms_of(backward[space])

        @pl.loop(0, count)
        def _(i):
            flat = pl.ds(i * chunk, chunk)
            for layer in range(layers + 2):
                for comp in range(3):
                    for dz in (-1, 0, 1):
                        terms = [
                            term
                            for term in table[comp]
                            if term[2] == dz and 0 <= layer - 1 + term[0] < layers
                        ]
                        if terms:
                            def load(dx, dy, dz, column):
                                return sec[column, layer - 1 + dx, at(i, dy), :]

                            value = weighted(terms, load)
                            if space > 0:
                                value = value + b[dz + 1, layer, comp, flat, :]
                            b[dz + 1, layer, comp, flat, :] = value
                        elif space == 0:
                            b[dz + 1, layer, comp, flat, :] = jnp.zeros((chunk, width), jnp.float32)


def finish(b, layers, rows, width, store):
    chunk = 16
    lane = lax.broadcasted_iota(jnp.int32, (chunk, width), 1)

    @pl.loop(0, (layers + 2) * 3)
    def _(plane):
        layer, comp = plane // 3, plane % 3

        @pl.loop(0, rows // chunk)
        def _(i):
            flat = pl.ds(i * chunk, chunk)
            before = pltpu.roll(b[0, layer, comp, flat, :], 1, 1)
            after = pltpu.roll(b[2, layer, comp, flat, :], width - 1, 1)
            own = b[1, layer, comp, flat, :]
            own = own + jnp.where(lane == 0, 0.0, before) + jnp.where(lane == width - 1, 0.0, after)
            store(layer, comp, flat, own, jnp.where(lane == 0, before, after))


def kernel(blocks, groups, weights, inverse, m_in, mh_in, c, ch, own_ref, out_ref, m, mh, mz, mhz, f, rs, inv, sec, b):
    layers, tall, width = m.shape[0] - 4, m.shape[2], m.shape[3]
    rows = tall - 2 * PAD
    block, group = lax.axis_index("blk"), lax.axis_index("grp")
    edges = (block == 0, block == blocks - 1, group == 0, group == groups - 1)

    @pl.loop(0, (layers + 4) * 3)
    def _(plane):
        layer, comp = plane // 3, plane % 3
        m[layer, comp, pl.ds(PAD, rows), :] = m_in[layer, comp]
        mh[layer, comp, pl.ds(PAD, rows), :] = mh_in[layer, comp]

    compute(weights, inverse, m, mh, c, ch, mz, mhz, f, rs, inv, sec, b, edges, layers, tall)

    def store(layer, comp, flat, own, outside):
        own_ref[layer, comp, flat, :] = own
        out_ref[layer, comp, flat, :] = outside

    finish(b, layers, rows, width, store)


def shift(value, axis, step):
    count = lax.axis_size(axis)
    pairs = [(i, i + step) for i in range(count) if 0 <= i + step < count]
    return lax.ppermute(value, axis, pairs)


def local(residual, face_mask, conductivity, stencil):
    groups, blocks = lax.axis_size("grp"), lax.axis_size("blk")
    mask_float = face_mask.astype(jnp.float32)
    masked = jnp.swapaxes(residual * mask_float, 0, 1)
    layers, _, rows, width = masked.shape
    tall = rows + 2 * PAD
    low = shift(jnp.concatenate([masked[layers - 2, 1:], masked[layers - 1]]), "blk", 1)
    high = shift(jnp.concatenate([masked[0], masked[1, 1:]]), "blk", -1)
    coeff = conductivity[0].reshape(layers, rows, groups, width)
    coeff = lax.all_to_all(coeff.transpose(2, 0, 1, 3), "grp", 0, 0)
    low_c = shift(coeff[:, layers - 1], "blk", 1)
    high_c = shift(coeff[:, 0], "blk", -1)
    nought = jnp.zeros((1, rows, width), jnp.float32)
    m = jnp.concatenate([nought, low[:2], low[2:], masked.reshape(-1, rows, width), high[:3], nought, high[3:]])
    c = jnp.concatenate([low_c[:, None], coeff, high_c[:, None]], 1)
    flat_c = c.reshape(-1, rows, width)
    planes = m.shape[0]
    right = shift(jnp.concatenate([m[..., width - 2], m[..., width - 1], flat_c[..., width - 1]]), "grp", 1)
    left = shift(jnp.concatenate([m[..., 0], m[..., 1], flat_c[..., 0]]), "grp", -1)
    gap = jnp.zeros((planes, rows, width - 4), jnp.float32)
    mh = jnp.concatenate(
        [left[:planes, :, None], left[planes : 2 * planes, :, None], gap, right[:planes, :, None], right[planes : 2 * planes, :, None]],
        2,
    )
    gap = jnp.ones((flat_c.shape[0], rows, width - 2), jnp.float32)
    ch = jnp.concatenate([left[2 * planes :, :, None], gap, right[2 * planes :, :, None]], 2)
    weights = stencil.reshape(-1)
    inverse = (1.0 / jnp.diagonal(stencil[:, 13], axis1=1, axis2=2)).reshape(-1)

    smem, vmem = pl.BlockSpec(memory_space=pltpu.SMEM), pl.BlockSpec(memory_space=pltpu.VMEM)
    result = jax.ShapeDtypeStruct((layers + 2, 3, rows, width), jnp.float32)
    scratch = lambda *shape: pltpu.VMEM(shape, jnp.float32)
    own, outside = pl.pallas_call(
        lambda *refs: kernel(blocks, groups, *refs),
        out_shape=(result, result),
        in_specs=[smem, smem] + [vmem] * 4,
        out_specs=(vmem, vmem),
        scratch_shapes=[
            scratch(layers + 4, 3, tall, width),
            scratch(layers + 4, 3, tall, width),
            scratch(2, layers + 4, 3, tall, width),
            scratch(2, layers + 4, 3, tall, width),
            scratch(3, 3, layers + 2, tall, width),
            scratch(layers + 2, 3, rows, width),
            scratch(layers + 2, rows, width),
            scratch(3, layers, tall, width),
            scratch(3, layers + 2, 3, rows, width),
        ],
        compiler_params=pltpu.CompilerParams(vmem_limit_bytes=56 * 1024 * 1024),
        cost_estimate=pl.CostEstimate(flops=500 * 4 * layers * rows * width, bytes_accessed=8 << 20, transcendentals=0),
        name="smooth",
    )(weights, inverse, m.reshape(layers + 4, 3, rows, width), mh.reshape(layers + 4, 3, rows, width), c, ch.reshape(c.shape))

    to_right = shift(outside[..., 0], "grp", 1)
    to_left = shift(outside[..., width - 1], "grp", -1)
    column = jnp.arange(width)
    own = own + jnp.where(column == 0, to_right[..., None], 0.0) + jnp.where(column == width - 1, to_left[..., None], 0.0)
    from_low = shift(own[layers + 1, 1:], "blk", 1)
    from_high = shift(own[0, 1:], "blk", -1)
    total = own[1 : layers + 1]
    total = total.at[0, 1:].add(from_low).at[layers - 1, 1:].add(from_high)
    return jnp.swapaxes(total, 0, 1) * mask_float


def solution(mesh):
    return jax.shard_map(
        local,
        mesh=mesh,
        in_specs=(
            P(None, "blk", None, "grp"),
            P(None, "blk", None, "grp"),
            P("grp", "blk", None, None),
            P(),
        ),
        out_specs=P(None, "blk", None, "grp"),
        check_vma=False,
    )
```

time: 292 us -> 135 us (0.46)
  the two profiles are of different devices: /device:TPU:9 before, /device:TPU:6 now
where the time goes in v1:
time: 135 us; the launch traced here: 134 us
  Pallas kernels  46.8 us (35%)
  local copies, waits for them, and re-layouts  32.7 us (24%)
  starting transfers between devices  32.2 us (24%)
  waiting for transfers between devices  16.3 us (12%)
  other arithmetic  6.02 us (4%)
    pallas_call x1, Pallas kernels, local(): pl.pallas_call(lambda *refs: kernel(blocks, groups, *refs), out_shape=(re...  46.8 us
    ppermute x10, starting transfers between devices, shift(): return lax.ppermute(value, axis, pairs)  28.3 us
    ppermute x10, waiting for transfers between devices, shift(): return lax.ppermute(value, axis, pairs)  16 us
    concatenate x5, local copies, waits for them, and re-layouts, local(): jnp.concatenate([left[:planes, :, None], left[planes:2 * planes, :, None]...  10.1 us
    all_to_all x1, starting transfers between devices, local(): coeff = lax.all_to_all(coeff.transpose(2, 0, 1, 3), 'grp', 0, 0)  3.97 us
    concatenate x2, local copies, waits for them, and re-layouts, local(): jnp.concatenate([nought, low[:2], low[2:], masked.reshape(-1, rows, width...  3.69 us
    unnamed x20, local copies, waits for them, and re-layouts  3.34 us
    concatenate x1, other arithmetic, local(): jnp.concatenate([left[2 * planes:, :, None], gap, right[2 * planes:, :, N...  2.89 us
  transfers between devices with their start and end apart: 11, of which 7 were waited for; matrix products, arithmetic and copies ran while one was open for 10% of the time, Pallas kernels for 0%

profile of v1, /device:TPU:6, one launch (start us, length us, event | category | flops | bytes accessed | tf_op | source)
XLA Modules:
  0.0 134.5 jit_solution(4425556498376241755)
XLA Ops:
  0.0 1.2 copy.59
  1.2 0.0 copy-start.4
  1.3 1.0 copy.60
  2.3 4.0 %all-to-all-start = ((f32[4,2,128,128]{3,2,1,0:T(8,128)}), f32[4,2,128,128]{3,2,1,0:T(8,128)S(1)}, u32[]{:S(2)}, u32[]{:S(2)}) async-start(f32[4,2,128,128]{3,2,1,0:T(8,128)} %copy.60), calls=%async_computation | async-start | bytes 1048576 | tf_op jit(solution)/shard_map/all_to_all | solution.py:295
  6.3 0.0 copy-start.5
  6.4 3.4 %collective-permute-start = (f32[5,128,128]{2,1,0:T(8,128)S(1)}, f32[5,128,128]{2,1,0:T(8,128)S(1)}, u32[]{:S(2)}, u32[]{:S(2)}) collective-permute-start(f32[5,128,128]{2,1,0:T(8,128)S(1)} %pad_maximum_fusion.2), channel_id=1, source_target_pairs={{0,1},{1,2},{2,3},{3,4},{4,5},{5,6},{6,7},{8,9},{9,10},{10,11},{11... | collective-permute-start | bytes 983048 | tf_op jit(solution)/shard_map/ppermute | solution.py:283
  9.9 2.4 %collective-permute-start.1 = (f32[5,128,128]{2,1,0:T(8,128)S(1)}, f32[5,128,128]{2,1,0:T(8,128)S(1)}, u32[]{:S(2)}, u32[]{:S(2)}) collective-permute-start(f32[5,128,128]{2,1,0:T(8,128)S(1)} %pad_maximum_fusion.3), channel_id=1, source_target_pairs={{1,0},{2,1},{3,2},{4,3},{5,4},{6,5},{7,6},{9,8},{10,9},{11,10},{12... | collective-permute-start | bytes 983048 | tf_op jit(solution)/shard_map/ppermute | solution.py:283
  12.3 0.1 slice.147
  12.4 0.2 copy.76
  12.6 0.6 gather_fusion
  13.2 0.3 all-to-all-done
  13.4 0.8 slice_bitcast_fusion.1
  14.2 1.9 %collective-permute-start.3 = (f32[4,128,128]{2,1,0:T(8,128)}, f32[4,128,128]{2,1,0:T(8,128)}, u32[]{:S(2)}, u32[]{:S(2)}) collective-permute-start(f32[4,128,128]{2,1,0:T(8,128)} %get-tuple-element.44), channel_id=1, source_target_pairs={{1,0},{2,1},{3,2},{4,3},{5,4},{6,5},{7,6},{9,8},{10,9},{11,10},{12... | collective-permute-start | bytes 786440 | tf_op jit(solution)/shard_map/ppermute | solution.py:283
  16.2 4.8 %collective-permute-start.2 = (f32[4,128,128]{2,1,0:T(8,128)}, f32[4,128,128]{2,1,0:T(8,128)}, u32[]{:S(2)}, u32[]{:S(2)}) collective-permute-start(f32[4,128,128]{2,1,0:T(8,128)} %get-tuple-element.43), channel_id=1, source_target_pairs={{0,1},{1,2},{2,3},{3,4},{4,5},{5,6},{6,7},{8,9},{9,10},{10,11},{11... | collective-permute-start | bytes 786440 | tf_op jit(solution)/shard_map/ppermute | solution.py:283
  21.0 0.2 copy.48
  21.2 0.8 reshape.117.refs_0_
  22.0 0.1 copy.51
  22.1 0.6 div.8.refs_1_
  22.7 0.2 copy.55
  23.0 0.1 pad.9.clone
  23.0 0.3 collective-permute-done.1
  23.3 0.1 copy.56
  23.5 0.8 copy.57
  24.3 7.3 %collective-permute-done = f32[5,128,128]{2,1,0:T(8,128)S(1)} collective-permute-done((f32[5,128,128]{2,1,0:T(8,128)S(1)}, f32[5,128,128]{2,1,0:T(8,128)S(1)}, u32[]{:S(2)}, u32[]{:S(2)}) %collective-permute-start) | collective-permute-done | bytes 327712 | tf_op jit(solution)/shard_map/ppermute | solution.py:283
  31.5 0.2 copy.54
  31.8 2.3 %concatenate.51 = f32[18,128,128]{1,0,2:T(8,128)S(1)} concatenate(f32[1,128,128]{1,0,2:T(1,128)S(1)} %broadcast_in_dim.52, f32[5,128,128]{1,0,2:T(8,128)S(1)} %copy.54, f32[6,128,128]{1,0,2:T(8,128)S(1)} %copy.55, f32[3,128,128]{1,0,2:T(4,128)S(1)} %copy.56, f32[1,128,128]{1,0,2:T(1,128)S(1)} %broadcast_in_dim.52, f32[2,128,128]{1,0,2:T(2,128)} %copy.57), dimensions={0} | concatenate | bytes 2359296 | tf_op jit(solution)/shard_map/concatenate | solution.py:299
  34.1 1.4 %copy.58 = f32[18,128,128]{2,1,0:T(8,128)} copy(f32[18,128,128]{1,0,2:T(8,128)S(1)} %concatenate.51) | data formatting | bytes 2359296 | tf_op jit(solution)/shard_map/concatenate | solution.py:299
  35.5 0.9 collective-permute-done.2
  36.4 1.1 pad_maximum_fusion.refs_4_
  37.5 0.4 fusion.2
  37.9 0.6 copy-done
  38.5 0.3 copy.79
  38.9 1.9 %collective-permute-start.4 = (f32[52,128]{1,0:T(8,128)S(1)}, f32[52,128]{1,0:T(8,128)S(1)}, u32[]{:S(2)}, u32[]{:S(2)}) collective-permute-start(f32[52,128]{1,0:T(8,128)S(1)} %pad_maximum_fusion.4), channel_id=1, source_target_pairs={{8,0},{16,8},{24,16},{9,1},{17,9},{25,17},{10,2},{18,10},{26,18},{... | collective-permute-start | bytes 79880 | tf_op jit(solution)/shard_map/ppermute | solution.py:283
  40.8 0.3 copy.80
  41.2 2.4 %collective-permute-start.5 = (f32[52,128]{1,0:T(8,128)S(1)}, f32[52,128]{1,0:T(8,128)S(1)}, u32[]{:S(2)}, u32[]{:S(2)}) collective-permute-start(f32[52,128]{1,0:T(8,128)S(1)} %pad_maximum_fusion.5), channel_id=1, source_target_pairs={{0,8},{8,16},{16,24},{1,9},{9,17},{17,25},{2,10},{10,18},{18,26},{... | collective-permute-start | bytes 79880 | tf_op jit(solution)/shard_map/ppermute | solution.py:283
  43.6 0.6 copy-done.6
  44.2 1.0 concatenate.65
  45.2 1.0 concatenate.66
  46.2 0.1 collective-permute-done.5
  46.3 0.6 fusion.4
  46.9 0.0 copy-done.7
  47.0 1.7 %concatenate.67 = f32[6,3,128,1]{3,2,1,0:T(8,128)S(1)} reshape(f32[18,128]{1,0:T(8,128)} %get-tuple-element.50) | data formatting | bytes 18432 | tf_op jit(solution)/shard_map/concatenate | solution.py:306
  48.7 2.0 %concatenate.68 = f32[6,3,128,1]{3,2,1,0:T(8,128)} reshape(f32[18,128]{1,0:T(8,128)S(1)} %get-tuple-element.49) | data formatting | bytes 18432 | tf_op jit(solution)/shard_map/concatenate | solution.py:306
  50.7 0.7 slice.197
  51.4 1.4 %copy.70 = f32[4,4,128,1]{3,2,1,0:T(8,128)} copy(f32[4,4,128,1]{2,1,0,3:T(4,128)S(1)} %bitcast.69) | data formatting | bytes 16384 | tf_op jit(solution)/shard_map/concatenate | solution.py:311
  52.8 0.7 slice.196
  53.5 1.4 %copy.69 = f32[4,4,128,1]{3,2,1,0:T(8,128)} copy(f32[4,4,128,1]{2,1,0,3:T(4,128)S(1)} %bitcast.70) | data formatting | bytes 16384 | tf_op jit(solution)/shard_map/concatenate | solution.py:311
  54.8 2.9 %pad_maximum_fusion.1.refs_5_ = f32[4,4,128,128]{3,2,1,0:T(8,128)} fusion(f32[4,4,128,1]{3,2,1,0:T(8,128)} %copy.70, f32[4,4,128,1]{3,2,1,0:T(8,128)} %copy.69, f32[128]{0:T(128)S(1)} %pad.9.clone), kind=kLoop, calls=%fused_computation.2 | loop fusion | flops 524288 | bytes 1065472 | tf_op jit(solution)/shard_map/concatenate | solution.py:311
  57.7 1.2 broadcast_in_dim.55
  58.9 4.4 %concatenate.59.refs_3_ = f32[6,3,128,128]{3,2,1,0:T(8,128)} concatenate(f32[6,3,128,1]{3,2,1,0:T(8,128)S(1)} %concatenate.65, f32[6,3,128,1]{3,2,1,0:T(8,128)S(1)} %concatenate.66, f32[6,3,128,124]{3,2,1,0:T(8,128)} %broadcast_in_dim.55, f32[6,3,128,1]{3,2,1,0:T(8,128)S(1)} %concatenate.67, f32[6,3,128,1]{3,2,1,0:T(8,128)} %concatenate.68), dimensions={3} | concatenate | bytes 2359296 | tf_op jit(solution)/shard_map/concatenate | solution.py:306
  63.3 46.8 %smooth.1 = (f32[4,3,128,128]{3,2,1,0:T(8,128)}, f32[4,3,128,128]{3,2,1,0:T(8,128)}) custom-call(f32[972]{0:T(1024)} %reshape.117.refs_0_, f32[12]{0:T(128)} %div.8.refs_1_, f32[6,3,128,128]{3,2,1,0:T(8,128)} %bitcast.64, f32[6,3,128,128]{3,2,1,0:T(8,128)} %concatenate.59.refs_3_, f32[4,4,128,128]{3,2,1,0:T(8,128)} %copy-done, ...), custom_call_target="tpu_custom_call" | custom-call | flops 65536000 | bytes 8388608 | tf_op jit(solution)/shard_map/smooth/pallas_call | solution.py:318
  110.0 1.7 %fusion.3 = (f32[4,3,128,1]{3,2,1,0:T(8,128)S(1)}, f32[4,3,128,1]{3,2,1,0:T(8,128)S(1)}) fusion(f32[4,3,128,128]{3,2,1,0:T(8,128)} %get-tuple-element.32), kind=kLoop, calls=%fused_computation.32 | loop fusion | bytes 24576 | tf_op jit(solution)/shard_map/slice | solution.py:339
  111.7 0.3 copy.73
  112.0 3.0 %collective-permute-start.7 = (f32[4,3,128]{2,0,1:T(4,128)S(1)}, f32[4,3,128]{2,0,1:T(4,128)S(1)}, u32[]{:S(2)}, u32[]{:S(2)}) collective-permute-start(f32[4,3,128]{2,0,1:T(4,128)S(1)} %bitcast.71), channel_id=1, source_target_pairs={{8,0},{16,8},{24,16},{9,1},{17,9},{25,17},{10,2},{18,10},{26,18},{... | collective-permute-start | bytes 18440 | tf_op jit(solution)/shard_map/ppermute | solution.py:283
  115.0 0.3 copy.71
  115.3 1.9 %collective-permute-start.6 = (f32[4,3,128]{2,0,1:T(4,128)S(1)}, f32[4,3,128]{2,0,1:T(4,128)S(1)}, u32[]{:S(2)}, u32[]{:S(2)}) collective-permute-start(f32[4,3,128]{2,0,1:T(4,128)S(1)} %bitcast.72), channel_id=1, source_target_pairs={{0,8},{8,16},{16,24},{1,9},{9,17},{17,25},{2,10},{10,18},{18,26},{... | collective-permute-start | bytes 18440 | tf_op jit(solution)/shard_map/ppermute | solution.py:283
  117.2 3.0 %collective-permute-done.6 = f32[4,3,128]{2,0,1:T(4,128)S(1)} collective-permute-done((f32[4,3,128]{2,0,1:T(4,128)S(1)}, f32[4,3,128]{2,0,1:T(4,128)S(1)}, u32[]{:S(2)}, u32[]{:S(2)}) %collective-permute-start.6) | collective-permute-done | bytes 6176 | tf_op jit(solution)/shard_map/ppermute | solution.py:283
  120.2 0.5 select_add_fusion
  120.7 4.5 %collective-permute-start.8 = (f32[2,128,128]{2,1,0:T(8,128)S(1)}, f32[2,128,128]{2,1,0:T(8,128)S(1)}, u32[]{:S(2)}, u32[]{:S(2)}) collective-permute-start(f32[2,128,128]{2,1,0:T(8,128)S(1)} %get-tuple-element.40), channel_id=1, source_target_pairs={{0,1},{1,2},{2,3},{3,4},{4,5},{5,6},{6,7},{8,9},{9,10},{10,11},{11... | collective-permute-start | bytes 393224 | tf_op jit(solution)/shard_map/ppermute | solution.py:283
  125.2 0.6 fusion.6
  125.9 1.9 %collective-permute-start.9 = (f32[2,128,128]{2,1,0:T(8,128)S(1)}, f32[2,128,128]{2,1,0:T(8,128)S(1)}, u32[]{:S(2)}, u32[]{:S(2)}) collective-permute-start(f32[2,128,128]{2,1,0:T(8,128)S(1)} %get-tuple-element.39), channel_id=1, source_target_pairs={{1,0},{2,1},{3,2},{4,3},{5,4},{6,5},{7,6},{9,8},{10,9},{11,10},{12... | collective-permute-start | bytes 393224 | tf_op jit(solution)/shard_map/ppermute | solution.py:283
  127.8 1.4 %fusion.1 = f32[2,3,128,128]{3,2,1,0:T(8,128)S(1)} fusion(f32[2,3,128,128]{3,2,1,0:T(8,128)S(1)} %slice.198, s32[]{:T(128)} %bitcast.28, s32[]{:T(128)} %bitcast.29, f32[2,128,128]{2,1,0:T(8,128)S(1)} %collective-permute-done.8), kind=kLoop, calls=%fused_computation.20 | loop fusion | flops 32768 | bytes 393224 | tf_op jit(solution)/shard_map/scatter-add | solution.py:346
  129.2 4.5 %collective-permute-done.9 = f32[2,128,128]{2,1,0:T(8,128)S(1)} collective-permute-done((f32[2,128,128]{2,1,0:T(8,128)S(1)}, f32[2,128,128]{2,1,0:T(8,128)S(1)}, u32[]{:S(2)}, u32[]{:S(2)}) %collective-permute-start.9) | collective-permute-done | bytes 131104 | tf_op jit(solution)/shard_map/ppermute | solution.py:283
  133.7 0.8 copy.75
  (38 shorter events, 0.4 us)
Async XLA Ops:
  1.2 5.0 %copy-start.1 = (s32[3,2,128,128]{3,2,1,0:T(8,128)S(1)}, s32[3,2,128,128]{3,2,1,0:T(8,128)}, u32[]{:S(2)}) copy-start(s32[3,2,128,128]{3,2,1,0:T(8,128)} %param.9) | copy-start | bytes 1179652
  1.2 5.0 %copy-start.4 = (f32[3,2,128,128]{3,2,1,0:T(8,128)S(1)}, f32[3,2,128,128]{3,2,1,0:T(8,128)}, u32[]{:S(2)}) copy-start(f32[3,2,128,128]{3,2,1,0:T(8,128)} %param.8) | copy-start | bytes 1179652
  2.3 11.2 %all-to-all-start = ((f32[4,2,128,128]{3,2,1,0:T(8,128)}), f32[4,2,128,128]{3,2,1,0:T(8,128)S(1)}, u32[]{:S(2)}, u32[]{:S(2)}) async-start(f32[4,2,128,128]{3,2,1,0:T(8,128)} %copy.60), calls=%async_computation | async-start | bytes 1048576 | tf_op jit(solution)/shard_map/all_to_all | solution.py:295
  6.3 6.0 %copy-start.5 = (f32[4,27,3,3]{1,0,3,2:T(4,128)S(1)}, f32[4,27,3,3]{1,0,3,2:T(4,128)}, u32[]{:S(2)}) copy-start(f32[4,27,3,3]{1,0,3,2:T(4,128)} %param.11) | copy-start | bytes 11668
  6.4 25.1 %collective-permute-start = (f32[5,128,128]{2,1,0:T(8,128)S(1)}, f32[5,128,128]{2,1,0:T(8,128)S(1)}, u32[]{:S(2)}, u32[]{:S(2)}) collective-permute-start(f32[5,128,128]{2,1,0:T(8,128)S(1)} %pad_maximum_fusion.2), channel_id=1, source_target_pairs={{0,1},{1,2},{2,3},{3,4},{4,5},{5,6},{6,7},{8,9},{9,10},{10,11},{11... | collective-permute-start | bytes 983048 | tf_op jit(solution)/shard_map/ppermute | solution.py:283
  9.9 13.4 %collective-permute-start.1 = (f32[5,128,128]{2,1,0:T(8,128)S(1)}, f32[5,128,128]{2,1,0:T(8,128)S(1)}, u32[]{:S(2)}, u32[]{:S(2)}) collective-permute-start(f32[5,128,128]{2,1,0:T(8,128)S(1)} %pad_maximum_fusion.3), channel_id=1, source_target_pairs={{1,0},{2,1},{3,2},{4,3},{5,4},{6,5},{7,6},{9,8},{10,9},{11,10},{12... | collective-permute-start | bytes 983048 | tf_op jit(solution)/shard_map/ppermute | solution.py:283
  14.2 21.3 %collective-permute-start.3 = (f32[4,128,128]{2,1,0:T(8,128)}, f32[4,128,128]{2,1,0:T(8,128)}, u32[]{:S(2)}, u32[]{:S(2)}) collective-permute-start(f32[4,128,128]{2,1,0:T(8,128)} %get-tuple-element.44), channel_id=1, source_target_pairs={{1,0},{2,1},{3,2},{4,3},{5,4},{6,5},{7,6},{9,8},{10,9},{11,10},{12... | collective-permute-start | bytes 786440 | tf_op jit(solution)/shard_map/ppermute | solution.py:283
  16.2 20.2 %collective-permute-start.2 = (f32[4,128,128]{2,1,0:T(8,128)}, f32[4,128,128]{2,1,0:T(8,128)}, u32[]{:S(2)}, u32[]{:S(2)}) collective-permute-start(f32[4,128,128]{2,1,0:T(8,128)} %get-tuple-element.43), channel_id=1, source_target_pairs={{0,1},{1,2},{2,3},{3,4},{4,5},{5,6},{6,7},{8,9},{9,10},{10,11},{11... | collective-permute-start | bytes 786440 | tf_op jit(solution)/shard_map/ppermute | solution.py:283
  37.5 1.0 copy-start
  38.9 4.7 %collective-permute-start.4 = (f32[52,128]{1,0:T(8,128)S(1)}, f32[52,128]{1,0:T(8,128)S(1)}, u32[]{:S(2)}, u32[]{:S(2)}) collective-permute-start(f32[52,128]{1,0:T(8,128)S(1)} %pad_maximum_fusion.4), channel_id=1, source_target_pairs={{8,0},{16,8},{24,16},{9,1},{17,9},{25,17},{10,2},{18,10},{26,18},{... | collective-permute-start | bytes 79880 | tf_op jit(solution)/shard_map/ppermute | solution.py:283
  41.2 5.2 %collective-permute-start.5 = (f32[52,128]{1,0:T(8,128)S(1)}, f32[52,128]{1,0:T(8,128)S(1)}, u32[]{:S(2)}, u32[]{:S(2)}) collective-permute-start(f32[52,128]{1,0:T(8,128)S(1)} %pad_maximum_fusion.5), channel_id=1, source_target_pairs={{0,8},{8,16},{16,24},{1,9},{9,17},{17,25},{2,10},{10,18},{18,26},{... | collective-permute-start | bytes 79880 | tf_op jit(solution)/shard_map/ppermute | solution.py:283
  43.6 0.6 copy-start.6
  46.3 0.6 copy-start.7
  111.7 8.5 %copy-start.3 = (f32[4,3,128,128]{3,2,1,0:T(8,128)S(1)}, f32[4,3,128,128]{3,2,1,0:T(8,128)}, u32[]{:S(2)}) copy-start(f32[4,3,128,128]{3,2,1,0:T(8,128)} %get-tuple-element.31) | copy-start | bytes 2359300
  112.0 5.2 %collective-permute-start.7 = (f32[4,3,128]{2,0,1:T(4,128)S(1)}, f32[4,3,128]{2,0,1:T(4,128)S(1)}, u32[]{:S(2)}, u32[]{:S(2)}) collective-permute-start(f32[4,3,128]{2,0,1:T(4,128)S(1)} %bitcast.71), channel_id=1, source_target_pairs={{8,0},{16,8},{24,16},{9,1},{17,9},{25,17},{10,2},{18,10},{26,18},{... | collective-permute-start | bytes 18440 | tf_op jit(solution)/shard_map/ppermute | solution.py:283
  115.3 4.9 %collective-permute-start.6 = (f32[4,3,128]{2,0,1:T(4,128)S(1)}, f32[4,3,128]{2,0,1:T(4,128)S(1)}, u32[]{:S(2)}, u32[]{:S(2)}) collective-permute-start(f32[4,3,128]{2,0,1:T(4,128)S(1)} %bitcast.72), channel_id=1, source_target_pairs={{0,8},{8,16},{16,24},{1,9},{9,17},{17,25},{2,10},{10,18},{18,26},{... | collective-permute-start | bytes 18440 | tf_op jit(solution)/shard_map/ppermute | solution.py:283
  120.7 13.0 %copy-start.2 = (s32[3,2,128,128]{3,2,1,0:T(8,128)S(1)}, s32[3,2,128,128]{3,2,1,0:T(8,128)}, u32[]{:S(2)}) copy-start(s32[3,2,128,128]{3,2,1,0:T(8,128)} %param.9) | copy-start | bytes 1179652
  120.7 7.1 %collective-permute-start.8 = (f32[2,128,128]{2,1,0:T(8,128)S(1)}, f32[2,128,128]{2,1,0:T(8,128)S(1)}, u32[]{:S(2)}, u32[]{:S(2)}) collective-permute-start(f32[2,128,128]{2,1,0:T(8,128)S(1)} %get-tuple-element.40), channel_id=1, source_target_pairs={{0,1},{1,2},{2,3},{3,4},{4,5},{5,6},{6,7},{8,9},{9,10},{10,11},{11... | collective-permute-start | bytes 393224 | tf_op jit(solution)/shard_map/ppermute | solution.py:283
  125.9 7.8 %collective-permute-start.9 = (f32[2,128,128]{2,1,0:T(8,128)S(1)}, f32[2,128,128]{2,1,0:T(8,128)S(1)}, u32[]{:S(2)}, u32[]{:S(2)}) collective-permute-start(f32[2,128,128]{2,1,0:T(8,128)S(1)} %get-tuple-element.39), channel_id=1, source_target_pairs={{1,0},{2,1},{3,2},{4,3},{5,4},{6,5},{7,6},{9,8},{10,9},{11,10},{12... | collective-permute-start | bytes 393224 | tf_op jit(solution)/shard_map/ppermute | solution.py:283

commit v2 on v0

v2 whole, which is shorter than its diff:
```python
import jax
import jax.numpy as jnp
from jax import lax
from jax.experimental import pallas as pl
from jax.experimental.pallas import tpu as pltpu
from jax.sharding import PartitionSpec as P

OMEGA = 0.8
PAD = 8


def place_of(shift_x, shift_y, shift_z):
    return 9 * (shift_x + 1) + 3 * (shift_y + 1) + (shift_z + 1)


def blank_tables():
    return [
        [[[0.0, 0.0, 0.0] for row_one in range(3)] for place in range(27)] for space in range(4)
    ]


def restriction_tables():
    forward = blank_tables()
    centre = place_of(0, 0, 0)
    for comp in range(3):
        forward[0][centre][comp][comp] = 1.0
        others = [axis_one for axis_one in range(3) if axis_one != comp]
        for first_off in (0, -1):
            for second_off in (0, -1):
                vector = [0, 0, 0]
                vector[others[0]] = first_off
                vector[others[1]] = second_off
                forward[1][place_of(*vector)][comp][comp] += 0.25
        along_p = (comp + 1) % 3
        along_q = (comp + 2) % 3
        forward[2][centre][comp][along_q] += 1.0
        forward[2][centre][comp][along_p] -= 1.0
        vector = [0, 0, 0]
        vector[along_p] = -1
        forward[2][place_of(*vector)][comp][along_q] -= 1.0
        vector = [0, 0, 0]
        vector[along_q] = -1
        forward[2][place_of(*vector)][comp][along_p] += 1.0
    for comp in range(3):
        for shift_x in (-1, 0, 1):
            for shift_y in (-1, 0, 1):
                for shift_z in (-1, 0, 1):
                    source = list(forward[2][place_of(shift_x, shift_y, shift_z)][comp])
                    if abs(source[0]) + abs(source[1]) + abs(source[2]) == 0:
                        continue
                    vector = [shift_x, shift_y, shift_z]
                    vector[comp] += 1
                    for column in range(3):
                        forward[3][place_of(shift_x, shift_y, shift_z)][comp][column] += (
                            0.5 * source[column]
                        )
                        forward[3][place_of(*vector)][comp][column] += 0.5 * source[column]
    backward = blank_tables()
    for space in range(4):
        for shift_x in (-1, 0, 1):
            for shift_y in (-1, 0, 1):
                for shift_z in (-1, 0, 1):
                    for row_one in range(3):
                        for column in range(3):
                            backward[space][place_of(-shift_x, -shift_y, -shift_z)][row_one][
                                column
                            ] = forward[space][place_of(shift_x, shift_y, shift_z)][column][row_one]
    return (forward, backward)


MESH = pl.DeviceIdType.MESH


def terms_of(table):
    rows = [[] for comp in range(3)]
    for dx in (-1, 0, 1):
        for dy in (-1, 0, 1):
            for dz in (-1, 0, 1):
                for row in range(3):
                    for column in range(3):
                        weight = table[place_of(dx, dy, dz)][row][column]
                        if weight != 0.0:
                            rows[row].append((dx, dy, dz, column, weight))
    return rows


def weighted(terms, load):
    groups = {}
    for dx, dy, dz, column, weight in terms:
        piece = load(dx, dy, dz, column)
        held = groups.get(abs(weight))
        if held is None:
            groups[abs(weight)] = piece if weight > 0 else -piece
        else:
            groups[abs(weight)] = held + piece if weight > 0 else held - piece
    total = None
    for size, held in groups.items():
        held = held if size == 1.0 else held * size
        total = held if total is None else total + held
    return total


def ring(own, beside, step, lane):
    width = own.shape[-1]
    turn = 1 if step < 0 else width - 1
    edge = 0 if step < 0 else width - 1
    own_turned = pltpu.roll(own, turn, own.ndim - 1)
    beside_turned = pltpu.roll(beside, turn, own.ndim - 1)
    at_edge = lane == edge
    return (
        jnp.where(at_edge, beside_turned, own_turned),
        jnp.where(at_edge, own_turned, beside_turned),
    )


def first_stage(space, spots, forward, inverse, m, mh, c, ch, mz, mhz, f, rs, edges, layers, tall):
    first_block, last_block, first_lanes, last_lanes = edges
    rows, chunk, width = tall - 2 * PAD, 16, m.shape[-1]
    lane = lax.broadcasted_iota(jnp.int32, (chunk, width), 1)
    table = terms_of(forward[space])
    start, step, number = spots

    @pl.loop(0, number)
    def _(turn):
        layer = start + turn * step
        off = jnp.logical_or(
            jnp.logical_and(first_block, layer == 0),
            jnp.logical_and(last_block, layer == layers + 1),
        )
        off_left = jnp.logical_or(off, first_lanes).astype(jnp.int32)
        off_right = jnp.logical_or(off, last_lanes).astype(jnp.int32)

        @pl.loop(0, rows // chunk)
        def _(i):
            def at(shift=0):
                return pl.ds(i * chunk + (PAD + shift), chunk)

            flat = pl.ds(i * chunk, chunk)
            scale = OMEGA / c[space, layer, flat, :]
            scale_h = OMEGA / ch[space, layer, flat, :]
            for comp in range(3):
                def own(dx, dy, dz, column):
                    place = m if dz == 0 else mz.at[(dz + 1) // 2]
                    return place[layer + 1 + dx, column, at(dy), :]

                def beside(dx, dy, dz, column):
                    place = mh if dz == 0 else mhz.at[(dz + 1) // 2]
                    return place[layer + 1 + dx, column, at(dy), :]

                centre = inverse[space * 3 + comp]
                restricted = weighted(table[comp], own)
                rs[space, layer, comp, flat, :] = restricted
                value = jnp.where(off, 0.0, restricted * (scale * centre))
                value_h = weighted(table[comp], beside) * (scale_h * centre)
                gone = jnp.where(lane == 0, off_right, off_left)
                value_h = jnp.where(gone != 0, 0.0, value_h)
                f[space, 1, comp, layer, at(), :] = value
                f[space, 0, comp, layer, at(), :] = ring(value, value_h, -1, lane)[0]
                f[space, 2, comp, layer, at(), :] = ring(value, value_h, 1, lane)[0]


def second_stage(space, backward, weights, inverse, c, f, rs, sec, b, layers, tall):
    rows, chunk, width = tall - 2 * PAD, 16, c.shape[-1]
    base = space * 243

    @pl.loop(0, rows // chunk)
    def _(i):
        def at(shift=0):
            return pl.ds(i * chunk + (PAD + shift), chunk)

        flat = pl.ds(i * chunk, chunk)
        total = [[None] * 3 for layer in range(layers)]
        for dy in (-1, 0, 1):
            for dz in (-1, 0, 1):
                for column in range(3):
                    planes = [f[space, dz + 1, column, layer, at(dy), :] for layer in range(layers + 2)]
                    for dx in (-1, 0, 1):
                        for comp in range(3):
                            weight = weights[base + place_of(dx, dy, dz) * 9 + comp * 3 + column]
                            for layer in range(layers):
                                piece = planes[layer + 1 + dx] * weight
                                held = total[layer][comp]
                                total[layer][comp] = piece if held is None else held + piece
        for layer in range(layers):
            coeff = c[space, layer + 1, flat, :]
            scale = OMEGA / coeff
            for comp in range(3):
                left = rs[space, layer + 1, comp, flat, :] - coeff * total[layer][comp]
                value = f[space, 1, comp, layer + 1, at(), :]
                sec[comp, layer, at(), :] = value + left * (scale * inverse[space * 3 + comp])

    table = terms_of(backward[space])

    @pl.loop(0, rows // chunk)
    def _(i):
        def at(shift=0):
            return pl.ds(i * chunk + (PAD + shift), chunk)

        flat = pl.ds(i * chunk, chunk)
        for layer in range(layers + 2):
            for comp in range(3):
                for dz in (-1, 0, 1):
                    terms = [
                        term
                        for term in table[comp]
                        if term[2] == dz and 0 <= layer - 1 + term[0] < layers
                    ]
                    if terms:
                        def load(dx, dy, dz, column):
                            return sec[column, layer - 1 + dx, at(dy), :]

                        value = weighted(terms, load)
                        if space > 0:
                            value = value + b[dz + 1, layer, comp, flat, :]
                        b[dz + 1, layer, comp, flat, :] = value
                    elif space == 0:
                        b[dz + 1, layer, comp, flat, :] = jnp.zeros((chunk, width), jnp.float32)


def kernel(
    weights, inverse, residual, mask, cond, out,
    m, mh, mz, mhz, c, ch, f, rs, sec, b,
    m_out, m_got, c_out, c_got, turned, sums, x_got, l_out, l_got,
    send_m, got_m, send_s, got_s, send_c, got_c, send_t, got_t, send_x, got_x, send_l, got_l,
):
    groups, blocks = lax.axis_size("grp"), lax.axis_size("blk")
    group, block = lax.axis_index("grp"), lax.axis_index("blk")
    layers, tall, width = m.shape[0] - 4, m.shape[2], m.shape[3]
    rows, chunk = tall - 2 * PAD, 16
    body = pl.ds(PAD, rows)
    lane = lax.broadcasted_iota(jnp.int32, (chunk, width), 1)
    edges = (block == 0, block == blocks - 1, group == 0, group == groups - 1)
    forward, backward = restriction_tables()

    def there(db):
        return jnp.logical_and(block + db >= 0, block + db < blocks)

    def beside(dg):
        return jnp.logical_and(group + dg >= 0, group + dg < groups)

    zeros = jnp.zeros((PAD, width), jnp.float32)
    plane_zeros = jnp.zeros((rows, width), jnp.float32)
    for layer in (0, 1, layers + 2, layers + 3):
        for comp in range(3):
            m[layer, comp, body, :] = plane_zeros
    m_got[...] = jnp.zeros_like(m_got)
    c_got[...] = jnp.ones_like(c_got)
    l_got[...] = jnp.zeros_like(l_got)
    x_got[...] = jnp.zeros_like(x_got)
    c[:, 0] = jnp.ones((4, rows, width), jnp.float32)
    c[:, layers + 1] = jnp.ones((4, rows, width), jnp.float32)

    barrier = pltpu.get_barrier_semaphore()
    for db in (-1, 0, 1):
        for turn in range(groups):
            if db == 0 and turn == 0:
                continue

            @pl.when(there(db))
            def _():
                pl.semaphore_signal(
                    barrier,
                    inc=1,
                    device_id=(lax.rem(group + turn, groups), block + db),
                    device_id_type=MESH,
                )

    for layer in range(layers):
        for comp in range(3):
            value = residual[comp, layer] * mask[comp, layer].astype(jnp.float32)
            m[layer + 2, comp, body, :] = value
            flipped = value.T
            m_out[0, layer, pl.ds(2 * comp, 2), :] = flipped[width - 2 :]
            m_out[1, layer, pl.ds(2 * comp, 2), :] = flipped[:2]
    c_out[...] = jnp.ones_like(c_out)
    for layer in range(layers):
        for part in range(groups):
            flipped = cond[0, layer, :, pl.ds(part * width, width)].T
            if part + 1 < groups:
                c_out[part + 1, pl.ds(2 * layer, 1), :] = flipped[width - 1 :]
            if part > 0:
                c_out[part - 1, pl.ds(2 * layer + 1, 1), :] = flipped[:1]

    neighbours = jnp.where(block > 0, groups, 0) + jnp.where(block < blocks - 1, groups, 0) + groups - 1
    pl.semaphore_wait(barrier, neighbours)

    def remote(src, dst, send, got, dg, db):
        return pltpu.make_async_remote_copy(
            src_ref=src,
            dst_ref=dst,
            send_sem=send,
            recv_sem=got,
            device_id=(lax.rem(group + dg + groups, groups), block + db),
            device_id_type=MESH,
        )

    two = pl.ds(1, 2)
    masked_copies = []
    for side, db in enumerate((1, -1)):
        near, far = (layers + 1, layers) if db > 0 else (2, 3)
        near_to, far_to = (1, 0) if db > 0 else (layers + 2, layers + 3)
        masked_copies.append((db, 0, remote(m.at[near, :, body], m.at[near_to, :, body], send_m.at[side, 0], got_m.at[side, 0], 0, db)))
        masked_copies.append((db, 0, remote(m.at[far, two, body], m.at[far_to, two, body], send_m.at[side, 1], got_m.at[side, 1], 0, db)))
    for place, db in enumerate((1, 0, -1)):
        for side, dg in enumerate((1, -1)):
            masked_copies.append((db, dg, remote(m_out.at[side], m_got.at[side, pl.ds(place * layers, layers)], send_s.at[place, side], got_s.at[place, side], dg, db)))
    near_copies, far_copies = [], []
    for place, db in enumerate((1, 0, -1)):
        for turn in range(groups):
            if db == 0 and turn == 0:
                continue
            target = lax.rem(group + turn, groups)
            part = pl.ds(pl.multiple_of(target * width, width), width)
            if db == 0:
                src, dst = cond.at[0, :, :, part], c.at[group, pl.ds(1, layers)]
            elif db > 0:
                src, dst = cond.at[0, pl.ds(layers - 1, 1), :, part], c.at[group, pl.ds(0, 1)]
            else:
                src, dst = cond.at[0, pl.ds(0, 1), :, part], c.at[group, pl.ds(layers + 1, 1)]
            held = near_copies if db == 0 else far_copies
            held.append((db, 0, remote(c_out.at[target], c_got.at[place, group], send_t.at[place, turn], got_t.at[place, turn], turn, db)))
            held.append((db, 0, remote(src, dst, send_c.at[place, turn], got_c.at[place, turn], turn, db)))

    def guarded(db, dg, act):
        if db == 0 and dg == 0:
            act()
        else:
            pl.when(jnp.logical_and(there(db), beside(dg)))(act)

    def start(copies):
        for db, dg, copy in copies:
            guarded(db, dg, copy.start)

    def arrive(copies):
        for db, dg, copy in copies:
            guarded(-db, -dg, copy.wait_recv)

    def sent(copies):
        for db, dg, copy in copies:
            guarded(db, dg, copy.wait_send)

    start(masked_copies)
    start(near_copies)
    start(far_copies)

    own_part = pl.ds(pl.multiple_of(group * width, width), width)
    c[group, pl.ds(1, layers)] = cond[0, :, :, own_part]
    c_got[1, group] = c_out[group]
    for side in (0, 1):
        edge = pl.ds(side * (rows + PAD), PAD)
        for layer in range(layers + 4):
            for comp in range(3):
                m[layer, comp, edge, :] = zeros
                mh[layer, comp, edge, :] = zeros
                for dz in (0, 1):
                    mz[dz, layer, comp, edge, :] = zeros
                    mhz[dz, layer, comp, edge, :] = zeros
        for comp in range(3):
            for layer in range(layers + 2):
                for dz in range(3):
                    for space in range(4):
                        f[space, dz, comp, layer, edge, :] = zeros
            for layer in range(layers):
                sec[comp, layer, edge, :] = zeros

    arrive(masked_copies)
    span = (layers + 4) * 8
    tail = jnp.zeros((width - 2 * span, rows), jnp.float32)
    turned[...] = jnp.concatenate([m_got[0].reshape(span, rows), m_got[1].reshape(span, rows), tail]).T

    @pl.loop(0, (layers + 4) * 3)
    def _(plane):
        layer, comp = plane // 3, plane % 3
        spot = layer * 8 + comp * 2

        @pl.loop(0, rows // chunk)
        def _(i):
            at = pl.ds(i * chunk + PAD, chunk)
            strips = turned[pl.ds(i * chunk, chunk), :]
            before = pltpu.roll(strips, width - 2 - spot, 1)
            after = pltpu.roll(strips, width - span - spot, 1)
            outer = jnp.where(lane < 2, after, jnp.where(lane >= width - 2, before, 0.0))
            own = m[layer, comp, at, :]
            mh[layer, comp, at, :] = outer
            for dz in (0, 1):
                one, other = ring(own, outer, 2 * dz - 1, lane)
                mz[dz, layer, comp, at, :] = one
                mhz[dz, layer, comp, at, :] = other

    def place_lanes(places, spots):
        held = 4 * 8
        tail = jnp.ones((width - held * len(places), rows), jnp.float32)
        turned[...] = jnp.concatenate([c_got[place].reshape(held, rows) for place in places] + [tail]).T
        for space in range(4):
            for spot in spots:
                row = space * 8 + (2 * layers - 2 if spot == 0 else held if spot == layers + 1 else 2 * (spot - 1))

                @pl.loop(0, rows // chunk)
                def _(i):
                    flat = pl.ds(i * chunk, chunk)
                    strips = turned[flat, :]
                    before = pltpu.roll(strips, (2 * width - 1 - row) % width, 1)
                    after = pltpu.roll(strips, (2 * width - 1 - row) % width, 1)
                    ch[space, spot, flat, :] = jnp.where(lane == 0, after, jnp.where(lane == width - 1, before, 1.0))

    arrive(near_copies)
    place_lanes((1,), range(1, layers + 1))
    for space in range(4):
        first_stage(space, (1, 1, layers), forward, inverse, m, mh, c, ch, mz, mhz, f, rs, edges, layers, tall)
    arrive(far_copies)
    place_lanes((0, 2), (0, layers + 1))
    for space in range(4):
        first_stage(space, (0, layers + 1, 2), forward, inverse, m, mh, c, ch, mz, mhz, f, rs, edges, layers, tall)
        second_stage(space, backward, weights, inverse, c, f, rs, sec, b, layers, tall)

    @pl.loop(0, rows // chunk)
    def _(i):
        flat = pl.ds(i * chunk, chunk)
        packed = jnp.zeros((chunk, width), jnp.float32)
        for layer in range(layers + 2):
            for comp in range(3):
                before = pltpu.roll(b[0, layer, comp, flat, :], 1, 1)
                after = pltpu.roll(b[2, layer, comp, flat, :], width - 1, 1)
                own = b[1, layer, comp, flat, :]
                own = own + jnp.where(lane == 0, 0.0, before) + jnp.where(lane == width - 1, 0.0, after)
                sums[layer, comp, flat, :] = own
                spot = comp if layer == 0 else 16 + comp if layer == layers + 1 else 8 + (layer - 1) * 3 + comp
                packed = jnp.where(lane == spot, before[:, :1], packed)
                packed = jnp.where(lane == 24 + spot, after[:, width - 1 :], packed)
        turned[flat, :] = packed
    flipped = turned[...].T
    l_out[...] = flipped[:48].reshape(2, 3, 8, rows)

    last_copies = []
    for side, db in enumerate((1, -1)):
        layer = layers + 1 if db > 0 else 0
        last_copies.append((db, 0, remote(sums.at[layer, two], x_got.at[side], send_x.at[side], got_x.at[side], 0, db)))
    for place, db in enumerate((-1, 0, 1)):
        for side, dg in enumerate((1, -1)):
            last_copies.append((db, dg, remote(l_out.at[side, place], l_got.at[side, place], send_l.at[place, side], got_l.at[place, side], dg, db)))
    start(last_copies)
    sent(masked_copies)
    sent(near_copies)
    sent(far_copies)
    arrive(last_copies)
    tail = jnp.zeros((width - 48, rows), jnp.float32)
    turned[...] = jnp.concatenate([l_got[...].reshape(48, rows), tail]).T

    @pl.loop(0, rows // chunk)
    def _(i):
        flat = pl.ds(i * chunk, chunk)
        strips = turned[flat, :]
        for layer in range(layers):
            for comp in range(3):
                total = sums[layer + 1, comp, flat, :]
                if comp > 0 and layer == 0:
                    total = total + x_got[0, comp - 1, flat, :]
                if comp > 0 and layer == layers - 1:
                    total = total + x_got[1, comp - 1, flat, :]
                spot = 8 + layer * 3 + comp
                low, high = strips[:, spot : spot + 1], strips[:, 24 + spot : 25 + spot]
                if layer == layers - 1:
                    low, high = low + strips[:, comp : comp + 1], high + strips[:, 24 + comp : 25 + comp]
                if layer == 0:
                    low, high = low + strips[:, 16 + comp : 17 + comp], high + strips[:, 40 + comp : 41 + comp]
                total = total + jnp.where(lane == 0, low, 0.0) + jnp.where(lane == width - 1, high, 0.0)
                out[comp, layer, flat, :] = total * mask[comp, layer, flat, :].astype(jnp.float32)
    sent(last_copies)


def local(residual, face_mask, conductivity, stencil):
    _, layers, rows, width = residual.shape
    groups = lax.axis_size("grp")
    tall = rows + 2 * PAD
    weights = stencil.reshape(-1)
    inverse = (1.0 / jnp.diagonal(stencil[:, 13], axis1=1, axis2=2)).reshape(-1)
    smem, vmem = pl.BlockSpec(memory_space=pltpu.SMEM), pl.BlockSpec(memory_space=pltpu.VMEM)
    scratch = lambda *shape: pltpu.VMEM(shape, jnp.float32)
    sems = lambda *shape: pltpu.SemaphoreType.DMA(shape)
    return pl.pallas_call(
        kernel,
        out_shape=jax.ShapeDtypeStruct(residual.shape, jnp.float32),
        in_specs=[smem, smem, vmem, vmem, vmem],
        out_specs=vmem,
        scratch_shapes=[
            scratch(layers + 4, 3, tall, width),
            scratch(layers + 4, 3, tall, width),
            scratch(2, layers + 4, 3, tall, width),
            scratch(2, layers + 4, 3, tall, width),
            scratch(4, layers + 2, rows, width),
            scratch(4, layers + 2, rows, width),
            scratch(4, 3, 3, layers + 2, tall, width),
            scratch(4, layers + 2, 3, rows, width),
            scratch(3, layers, tall, width),
            scratch(3, layers + 2, 3, rows, width),
            scratch(2, layers, 8, rows),
            scratch(2, layers + 4, 8, rows),
            scratch(groups, 8, rows),
            scratch(3, 4, 8, rows),
            scratch(rows, width),
            scratch(layers + 2, 3, rows, width),
            scratch(2, 2, rows, width),
            scratch(2, 3, 8, rows),
            scratch(2, 3, 8, rows),
            sems(2, 2), sems(2, 2), sems(3, 2), sems(3, 2), sems(3, groups), sems(3, groups),
            sems(3, groups), sems(3, groups), sems(2), sems(2), sems(3, 2), sems(3, 2),
        ],
        compiler_params=pltpu.CompilerParams(
            vmem_limit_bytes=60 * 1024 * 1024, collective_id=0, has_side_effects=True
        ),
        name="correct",
    )(weights, inverse, residual, face_mask, conductivity)


def solution(mesh):
    return jax.shard_map(
        local,
        mesh=mesh,
        in_specs=(
            P(None, "blk", None, "grp"),
            P(None, "blk", None, "grp"),
            P("grp", "blk", None, None),
            P(),
        ),
        out_specs=P(None, "blk", None, "grp"),
        check_vma=False,
    )
```

time: 292 us -> 103 us (0.35); the launches traced: 287 us -> 103 us
  waiting for transfers between devices: 150 us -> 0 us
  Pallas kernels: 0 us -> 97.9 us
  other arithmetic: 85.4 us -> 0.01 us
  starting transfers between devices: 18.8 us -> 0 us
  local copies, waits for them, and re-layouts: 19.8 us -> 5.03 us
  between operations: 13.9 us -> 0.03 us
    pallas_call x0 -> x1, Pallas kernels: none -> 97.9 us  [local(): pl.pallas_call(kernel, out_shape=jax.ShapeDtypeStruct(residual.shape, jnp...]
    ppermute x6 -> x0, waiting for transfers between devices: 95.2 us -> none  [the longest x3 86.5 us: extended(): lax.ppermute(lax.slice_in_dim(block, block.shape[dim] - width, None, axis...]
    reduce_sum x14 -> x0, other arithmetic: 42.3 us -> none  [dense_apply(): total = total + (block[:, :, None, None, None] * piece[None]).sum(1)]
    reduce_scatter x1 -> x0, waiting for transfers between devices: 32.5 us -> none  [local(): owned = lax.psum_scatter(prolonged, 'grp', scatter_dimension=3, tiled=True)]
    add x3 -> x0, other arithmetic: 25.1 us -> none  [the longest x1 14.3 us: local(): second = first + (restricted - applied) * scale]
    all_gather x1 -> x0, waiting for transfers between devices: 21.8 us -> none  [local(): whole = lax.all_gather(masked, 'grp', axis=3, tiled=True)]
    ppermute x6 -> x0, starting transfers between devices: 18.8 us -> none  [the longest x3 11.9 us: extended(): lax.ppermute(lax.slice_in_dim(block, 0, width, axis=dim), axis, backward)]
    slice x7 -> x1, local copies, waits for them, and re-layouts: 17.9 us -> 0.8 us  [local(): inverse = (1.0 / jnp.diagonal(stencil[:, 13], axis1=1, axis2=2)).reshape(-1)]
  transfers between devices with their start and end apart: 8 -> 0, of which waited for: 8 -> 0; matrix products, arithmetic and copies ran while one was open for 1% -> 0% of each run, Pallas kernels for 0% -> 0%
where the time goes in v2:
time: 103 us
  Pallas kernels  97.9 us (95%)
  local copies, waits for them, and re-layouts  5.03 us (5%)
    pallas_call x1, Pallas kernels, local(): pl.pallas_call(kernel, out_shape=jax.ShapeDtypeStruct(residual.shape, jnp...  97.9 us

profile of v2, /device:TPU:9, one launch (start us, length us, event | category | flops | bytes accessed | tf_op | source)
XLA Modules:
  0.0 103.0 jit_solution(12701028606150057577)
XLA Ops:
  0.0 0.8 slice.3
  0.8 0.2 copy.12
  1.0 0.0 copy-start
  1.0 0.6 gather_fusion
  1.6 0.1 copy.11
  1.7 0.6 div.8.inverse
  2.3 0.0 copy-done
  2.3 0.2 copy.8
  2.5 0.8 reshape.7.weights
  3.3 97.9 %correct.1 = f32[3,2,128,128]{3,2,1,0:T(8,128)} custom-call(f32[972]{0:T(1024)} %reshape.7.weights, f32[12]{0:T(128)} %div.8.inverse, f32[3,2,128,128]{3,2,1,0:T(8,128)} %residual.1, s32[3,2,128,128]{3,2,1,0:T(8,128)} %mask.1, f32[1,2,128,512]{3,2,1,0:T(8,128)} %cond.1), custom_call_target="tpu_custom_call" | custom-call | tf_op jit(solution)/shard_map/correct/pallas_call | solution.py:480
  101.2 1.8 %copy.14 = f32[3,2,128,128]{3,2,1,0:T(8,128)} copy(f32[3,2,128,128]{3,2,1,0:T(8,128)} %correct.1) | data formatting | bytes 786432
  (2 shorter events, 0.0 us)
Async XLA Ops:
  1.0 1.3 %copy-start = (f32[4,27,3,3]{1,0,3,2:T(4,128)S(1)}, f32[4,27,3,3]{1,0,3,2:T(4,128)}, u32[]{:S(2)}) copy-start(f32[4,27,3,3]{1,0,3,2:T(4,128)} %param.7) | copy-start | bytes 11668

commit v3 on v2

--- a/solution.py
+++ b/solution.py
@@ -113,12 +113,17 @@
     )
 
 
-def first_stage(space, spots, forward, inverse, m, mh, c, ch, mz, mhz, f, rs, edges, layers, tall):
+def inverse_of(weights, space, comp):
+    return 1.0 / weights[space * 243 + place_of(0, 0, 0) * 9 + comp * 4]
+
+
+def first_stage(space, spots, forward, weights, m, mh, c, ch, mz, mhz, f, rs, edges, layers, tall):
     first_block, last_block, first_lanes, last_lanes = edges
-    rows, chunk, width = tall - 2 * PAD, 16, m.shape[-1]
+    rows, chunk, width = tall - 2 * PAD, 64, m.shape[-1]
     lane = lax.broadcasted_iota(jnp.int32, (chunk, width), 1)
     table = terms_of(forward[space])
     start, step, number = spots
+    inverses = [inverse_of(weights, space, comp) for comp in range(3)]
 
     @pl.loop(0, number)
     def _(turn):
@@ -147,7 +152,7 @@
                     place = mh if dz == 0 else mhz.at[(dz + 1) // 2]
                     return place[layer + 1 + dx, column, at(dy), :]
 
-                centre = inverse[space * 3 + comp]
+                centre = inverses[comp]
                 restricted = weighted(table[comp], own)
                 rs[space, layer, comp, flat, :] = restricted
                 value = jnp.where(off, 0.0, restricted * (scale * centre))
@@ -159,9 +164,38 @@
                 f[space, 2, comp, layer, at(), :] = ring(value, value_h, 1, lane)[0]
 
 
-def second_stage(space, backward, weights, inverse, c, f, rs, sec, b, layers, tall):
+def dense(space, sources, i, weights, f, total, layers, chunk):
+    base = space * 243
+    for dy in (-1, 0, 1):
+        for dz in (-1, 0, 1):
+            for column in range(3):
+                for source in sources:
+                    plane = f[space, dz + 1, column, source, pl.ds(i * chunk + (PAD + dy), chunk), :]
+                    for layer in range(layers):
+                        dx = source - layer - 1
+                        if abs(dx) > 1:
+                            continue
+                        for comp in range(3):
+                            piece = plane * weights[base + place_of(dx, dy, dz) * 9 + comp * 3 + column]
+                            held = total[layer][comp]
+                            total[layer][comp] = piece if held is None else held + piece
+
+
+def near_stage(space, weights, f, part, layers, tall):
+    chunk = 16
+
+    @pl.loop(0, (tall - 2 * PAD) // chunk)
+    def _(i):
+        total = [[None] * 3 for layer in range(layers)]
+        dense(space, range(1, layers + 1), i, weights, f, total, layers, chunk)
+        for layer in range(layers):
+            for comp in range(3):
+                part[space, layer, comp, pl.ds(i * chunk, chunk), :] = total[layer][comp]
+
+
+def second_stage(space, backward, weights, c, f, rs, part, sec, b, layers, tall):
     rows, chunk, width = tall - 2 * PAD, 16, c.shape[-1]
-    base = space * 243
+    inverses = [inverse_of(weights, space, comp) for comp in range(3)]
 
     @pl.loop(0, rows // chunk)
     def _(i):
@@ -169,25 +203,15 @@
             return pl.ds(i * chunk + (PAD + shift), chunk)
 
         flat = pl.ds(i * chunk, chunk)
-        total = [[None] * 3 for layer in range(layers)]
-        for dy in (-1, 0, 1):
-            for dz in (-1, 0, 1):
-                for column in range(3):
-                    planes = [f[space, dz + 1, column, layer, at(dy), :] for layer in range(layers + 2)]
-                    for dx in (-1, 0, 1):
-                        for comp in range(3):
-                            weight = weights[base + place_of(dx, dy, dz) * 9 + comp * 3 + column]
-                            for layer in range(layers):
-                                piece = planes[layer + 1 + dx] * weight
-                                held = total[layer][comp]
-                                total[layer][comp] = piece if held is None else held + piece
+        total = [[part[space, layer, comp, flat, :] for comp in range(3)] for layer in range(layers)]
+        dense(space, (0, layers + 1), i, weights, f, total, layers, chunk)
         for layer in range(layers):
             coeff = c[space, layer + 1, flat, :]
             scale = OMEGA / coeff
             for comp in range(3):
                 left = rs[space, layer + 1, comp, flat, :] - coeff * total[layer][comp]
                 value = f[space, 1, comp, layer + 1, at(), :]
-                sec[comp, layer, at(), :] = value + left * (scale * inverse[space * 3 + comp])
+                sec[comp, layer, at(), :] = value + left * (scale * inverses[comp])
 
     table = terms_of(backward[space])
 
@@ -218,8 +242,8 @@
 
 
 def kernel(
-    weights, inverse, residual, mask, cond, out,
-    m, mh, mz, mhz, c, ch, f, rs, sec, b,
+    weights, residual, mask, cond, out,
+    m, mh, mz, mhz, c, ch, f, rs, partial, sec, b,
     m_out, m_got, c_out, c_got, turned, sums, x_got, l_out, l_got,
     send_m, got_m, send_s, got_s, send_c, got_c, send_t, got_t, send_x, got_x, send_l, got_l,
 ):
@@ -368,24 +392,22 @@
     tail = jnp.zeros((width - 2 * span, rows), jnp.float32)
     turned[...] = jnp.concatenate([m_got[0].reshape(span, rows), m_got[1].reshape(span, rows), tail]).T
 
+    tall_lane = lax.broadcasted_iota(jnp.int32, (rows, width), 1)
+
     @pl.loop(0, (layers + 4) * 3)
     def _(plane):
         layer, comp = plane // 3, plane % 3
         spot = layer * 8 + comp * 2
-
-        @pl.loop(0, rows // chunk)
-        def _(i):
-            at = pl.ds(i * chunk + PAD, chunk)
-            strips = turned[pl.ds(i * chunk, chunk), :]
-            before = pltpu.roll(strips, width - 2 - spot, 1)
-            after = pltpu.roll(strips, width - span - spot, 1)
-            outer = jnp.where(lane < 2, after, jnp.where(lane >= width - 2, before, 0.0))
-            own = m[layer, comp, at, :]
-            mh[layer, comp, at, :] = outer
-            for dz in (0, 1):
-                one, other = ring(own, outer, 2 * dz - 1, lane)
-                mz[dz, layer, comp, at, :] = one
-                mhz[dz, layer, comp, at, :] = other
+        strips = turned[...]
+        before = pltpu.roll(strips, width - 2 - spot, 1)
+        after = pltpu.roll(strips, width - span - spot, 1)
+        outer = jnp.where(tall_lane < 2, after, jnp.where(tall_lane >= width - 2, before, 0.0))
+        own = m[layer, comp, body, :]
+        mh[layer, comp, body, :] = outer
+        for dz in (0, 1):
+            one, other = ring(own, outer, 2 * dz - 1, tall_lane)
+            mz[dz, layer, comp, body, :] = one
+            mhz[dz, layer, comp, body, :] = other
 
     def place_lanes(places, spots):
         held = 4 * 8
@@ -394,24 +416,20 @@
         for space in range(4):
             for spot in spots:
                 row = space * 8 + (2 * layers - 2 if spot == 0 else held if spot == layers + 1 else 2 * (spot - 1))
-
-                @pl.loop(0, rows // chunk)
-                def _(i):
-                    flat = pl.ds(i * chunk, chunk)
-                    strips = turned[flat, :]
-                    before = pltpu.roll(strips, (2 * width - 1 - row) % width, 1)
-                    after = pltpu.roll(strips, (2 * width - 1 - row) % width, 1)
-                    ch[space, spot, flat, :] = jnp.where(lane == 0, after, jnp.where(lane == width - 1, before, 1.0))
+                strips = pltpu.roll(turned[...], (2 * width - 1 - row) % width, 1)
+                outermost = jnp.logical_or(tall_lane == 0, tall_lane == width - 1)
+                ch[space, spot] = jnp.where(outermost, strips, 1.0)
 
     arrive(near_copies)
     place_lanes((1,), range(1, layers + 1))
     for space in range(4):
-        first_stage(space, (1, 1, layers), forward, inverse, m, mh, c, ch, mz, mhz, f, rs, edges, layers, tall)
+        first_stage(space, (1, 1, layers), forward, weights, m, mh, c, ch, mz, mhz, f, rs, edges, layers, tall)
+        near_stage(space, weights, f, partial, layers, tall)
     arrive(far_copies)
     place_lanes((0, 2), (0, layers + 1))
     for space in range(4):
-        first_stage(space, (0, layers + 1, 2), forward, inverse, m, mh, c, ch, mz, mhz, f, rs, edges, layers, tall)
-        second_stage(space, backward, weights, inverse, c, f, rs, sec, b, layers, tall)
+        first_stage(space, (0, layers + 1, 2), forward, weights, m, mh, c, ch, mz, mhz, f, rs, edges, layers, tall)
+        second_stage(space, backward, weights, c, f, rs, partial, sec, b, layers, tall)
 
     @pl.loop(0, rows // chunk)
     def _(i):
@@ -473,14 +491,13 @@
     groups = lax.axis_size("grp")
     tall = rows + 2 * PAD
     weights = stencil.reshape(-1)
-    inverse = (1.0 / jnp.diagonal(stencil[:, 13], axis1=1, axis2=2)).reshape(-1)
     smem, vmem = pl.BlockSpec(memory_space=pltpu.SMEM), pl.BlockSpec(memory_space=pltpu.VMEM)
     scratch = lambda *shape: pltpu.VMEM(shape, jnp.float32)
     sems = lambda *shape: pltpu.SemaphoreType.DMA(shape)
     return pl.pallas_call(
         kernel,
         out_shape=jax.ShapeDtypeStruct(residual.shape, jnp.float32),
-        in_specs=[smem, smem, vmem, vmem, vmem],
+        in_specs=[smem, vmem, vmem, vmem],
         out_specs=vmem,
         scratch_shapes=[
             scratch(layers + 4, 3, tall, width),
@@ -491,6 +508,7 @@
             scratch(4, layers + 2, rows, width),
             scratch(4, 3, 3, layers + 2, tall, width),
             scratch(4, layers + 2, 3, rows, width),
+            scratch(4, layers, 3, rows, width),
             scratch(3, layers, tall, width),
             scratch(3, layers + 2, 3, rows, width),
             scratch(2, layers, 8, rows),
@@ -509,7 +527,7 @@
             vmem_limit_bytes=60 * 1024 * 1024, collective_id=0, has_side_effects=True
         ),
         name="correct",
-    )(weights, inverse, residual, face_mask, conductivity)
+    )(weights, residual, face_mask, conductivity)
 
 
 def solution(mesh):

time: 103 us -> 71.3 us (0.69)
  Pallas kernels: 97.9 us -> 67.6 us
  local copies, waits for them, and re-layouts: 5.03 us -> 3.49 us
    pallas_call x1, Pallas kernels: 97.9 us -> 67.6 us  [local(): pl.pallas_call(kernel, out_shape=jax.ShapeDtypeStruct(residual.shape, jnp...]
    unnamed x4 -> x2, local copies, waits for them, and re-layouts: 1.96 us -> 2.68 us
where the time goes in v3:
time: 71.3 us; the launch traced here: 71.1 us
  Pallas kernels  67.6 us (95%)
  local copies, waits for them, and re-layouts  3.49 us (5%)
    pallas_call x1, Pallas kernels, local(): pl.pallas_call(kernel, out_shape=jax.ShapeDtypeStruct(residual.shape, jnp...  67.6 us
    unnamed x2, local copies, waits for them, and re-layouts  2.68 us

profile of v3, /device:TPU:9, one launch (start us, length us, event | category | flops | bytes accessed | tf_op | source)
XLA Modules:
  0.0 71.1 jit_solution(5406274094996325205)
XLA Ops:
  0.0 0.9 %copy.5 = f32[4,27,3,3]{3,2,1,0:T(4,128)S(1)} copy(f32[4,27,3,3]{1,0,3,2:T(4,128)} %param.7) | data formatting | bytes 7776 | tf_op args[3]
  0.9 0.8 %reshape.3.weights = f32[972]{0:T(1024)} reshape(f32[4,27,3,3]{3,2,1,0:T(4,128)S(1)} %copy.5) | data formatting | bytes 7776 | tf_op jit(solution)/shard_map/reshape | solution.py:493
  1.7 67.6 %correct.1 = f32[3,2,128,128]{3,2,1,0:T(8,128)} custom-call(f32[972]{0:T(1024)} %reshape.3.weights, f32[3,2,128,128]{3,2,1,0:T(8,128)} %residual.1, s32[3,2,128,128]{3,2,1,0:T(8,128)} %mask.1, f32[1,2,128,512]{3,2,1,0:T(8,128)} %cond.1), custom_call_target="tpu_custom_call" | custom-call | tf_op jit(solution)/shard_map/correct/pallas_call | solution.py:497
  69.3 1.8 %copy.7 = f32[3,2,128,128]{3,2,1,0:T(8,128)} copy(f32[3,2,128,128]{3,2,1,0:T(8,128)} %correct.1) | data formatting | bytes 786432

commit v4 on v3

--- a/solution.py
+++ b/solution.py
@@ -181,13 +181,17 @@
                             total[layer][comp] = piece if held is None else held + piece
 
 
-def near_stage(space, weights, f, part, layers, tall):
+def near_stage(space, sources, fresh, weights, f, part, layers, tall):
     chunk = 16
 
     @pl.loop(0, (tall - 2 * PAD) // chunk)
     def _(i):
-        total = [[None] * 3 for layer in range(layers)]
-        dense(space, range(1, layers + 1), i, weights, f, total, layers, chunk)
+        flat = pl.ds(i * chunk, chunk)
+        total = [
+            [None if fresh else part[space, layer, comp, flat, :] for comp in range(3)]
+            for layer in range(layers)
+        ]
+        dense(space, sources, i, weights, f, total, layers, chunk)
         for layer in range(layers):
             for comp in range(3):
                 part[space, layer, comp, pl.ds(i * chunk, chunk), :] = total[layer][comp]
@@ -319,7 +323,7 @@
         )
 
     two = pl.ds(1, 2)
-    masked_copies = []
+    masked_copies, lane_copies = [], []
     for side, db in enumerate((1, -1)):
         near, far = (layers + 1, layers) if db > 0 else (2, 3)
         near_to, far_to = (1, 0) if db > 0 else (layers + 2, layers + 3)
@@ -327,7 +331,8 @@
         masked_copies.append((db, 0, remote(m.at[far, two, body], m.at[far_to, two, body], send_m.at[side, 1], got_m.at[side, 1], 0, db)))
     for place, db in enumerate((1, 0, -1)):
         for side, dg in enumerate((1, -1)):
-            masked_copies.append((db, dg, remote(m_out.at[side], m_got.at[side, pl.ds(place * layers, layers)], send_s.at[place, side], got_s.at[place, side], dg, db)))
+            held = lane_copies if db == 0 else masked_copies
+            held.append((db, dg, remote(m_out.at[side], m_got.at[side, pl.ds(place * layers, layers)], send_s.at[place, side], got_s.at[place, side], dg, db)))
     near_copies, far_copies = [], []
     for place, db in enumerate((1, 0, -1)):
         for turn in range(groups):
@@ -363,6 +368,7 @@
         for db, dg, copy in copies:
             guarded(db, dg, copy.wait_send)
 
+    start(lane_copies)
     start(masked_copies)
     start(near_copies)
     start(far_copies)
@@ -387,17 +393,19 @@
             for layer in range(layers):
                 sec[comp, layer, edge, :] = zeros
 
-    arrive(masked_copies)
-    span = (layers + 4) * 8
-    tail = jnp.zeros((width - 2 * span, rows), jnp.float32)
-    turned[...] = jnp.concatenate([m_got[0].reshape(span, rows), m_got[1].reshape(span, rows), tail]).T
+    span = layers * 8
 
     tall_lane = lax.broadcasted_iota(jnp.int32, (rows, width), 1)
 
-    @pl.loop(0, (layers + 4) * 3)
-    def _(plane):
-        layer, comp = plane // 3, plane % 3
-        spot = layer * 8 + comp * 2
+    def widen(start):
+        tail = jnp.zeros((width - 2 * span, rows), jnp.float32)
+        strips = [m_got[side, pl.ds(start, layers)].reshape(span, rows) for side in (0, 1)]
+        turned[...] = jnp.concatenate(strips + [tail]).T
+        pl.loop(0, layers * 3)(lambda plane: widen_plane(start, plane))
+
+    def widen_plane(start, plane):
+        layer, comp = start + plane // 3, plane % 3
+        spot = (plane // 3) * 8 + comp * 2
         strips = turned[...]
         before = pltpu.roll(strips, width - 2 - spot, 1)
         after = pltpu.roll(strips, width - span - spot, 1)
@@ -420,11 +428,28 @@
                 outermost = jnp.logical_or(tall_lane == 0, tall_lane == width - 1)
                 ch[space, spot] = jnp.where(outermost, strips, 1.0)
 
+    whole = tuple(range(1, layers + 1))
+
+    def first(space, start, number):
+        first_stage(space, (start, 1, number), forward, weights, m, mh, c, ch, mz, mhz, f, rs, edges, layers, tall)
+
+    arrive(lane_copies)
+    widen(2)
     arrive(near_copies)
-    place_lanes((1,), range(1, layers + 1))
-    for space in range(4):
-        first_stage(space, (1, 1, layers), forward, weights, m, mh, c, ch, mz, mhz, f, rs, edges, layers, tall)
-        near_stage(space, weights, f, partial, layers, tall)
+    place_lanes((1,), whole)
+    first(0, 1, layers)
+    near_stage(0, whole, True, weights, f, partial, layers, tall)
+    for space in (1, 2):
+        first(space, 2, layers - 1)
+        near_stage(space, whole[1:], True, weights, f, partial, layers, tall)
+    arrive(masked_copies)
+    widen(0)
+    widen(layers + 2)
+    for space in (1, 2):
+        first(space, 1, 1)
+        near_stage(space, whole[:1], False, weights, f, partial, layers, tall)
+    first(3, 1, layers)
+    near_stage(3, whole, True, weights, f, partial, layers, tall)
     arrive(far_copies)
     place_lanes((0, 2), (0, layers + 1))
     for space in range(4):
@@ -457,6 +482,7 @@
         for side, dg in enumerate((1, -1)):
             last_copies.append((db, dg, remote(l_out.at[side, place], l_got.at[side, place], send_l.at[place, side], got_l.at[place, side], dg, db)))
     start(last_copies)
+    sent(lane_copies)
     sent(masked_copies)
     sent(near_copies)
     sent(far_copies)

time: 71.3 us -> 64.5 us (0.905)
  Pallas kernels: 67.6 us -> 60.7 us
    pallas_call x1, Pallas kernels: 67.6 us -> 60.7 us  [local(): pl.pallas_call(kernel, out_shape=jax.ShapeDtypeStruct(residual.shape, jnp...]
where the time goes in v4:
time: 64.5 us; the launch traced here: 64.2 us
  Pallas kernels  60.7 us (94%)
  local copies, waits for them, and re-layouts  3.49 us (5%)
    pallas_call x1, Pallas kernels, local(): pl.pallas_call(kernel, out_shape=jax.ShapeDtypeStruct(residual.shape, jnp...  60.7 us
    unnamed x2, local copies, waits for them, and re-layouts  2.68 us

profile of v4, /device:TPU:9, one launch (start us, length us, event | category | flops | bytes accessed | tf_op | source)
XLA Modules:
  0.0 64.2 jit_solution(7651736905904955666)
XLA Ops:
  0.0 0.9 %copy.5 = f32[4,27,3,3]{3,2,1,0:T(4,128)S(1)} copy(f32[4,27,3,3]{1,0,3,2:T(4,128)} %param.7) | data formatting | bytes 7776 | tf_op args[3]
  0.9 0.8 %reshape.3.weights = f32[972]{0:T(1024)} reshape(f32[4,27,3,3]{3,2,1,0:T(4,128)S(1)} %copy.5) | data formatting | bytes 7776 | tf_op jit(solution)/shard_map/reshape | solution.py:519
  1.7 60.7 %correct.1 = f32[3,2,128,128]{3,2,1,0:T(8,128)} custom-call(f32[972]{0:T(1024)} %reshape.3.weights, f32[3,2,128,128]{3,2,1,0:T(8,128)} %residual.1, s32[3,2,128,128]{3,2,1,0:T(8,128)} %mask.1, f32[1,2,128,512]{3,2,1,0:T(8,128)} %cond.1), custom_call_target="tpu_custom_call" | custom-call | tf_op jit(solution)/shard_map/correct/pallas_call | solution.py:523
  62.5 1.8 %copy.7 = f32[3,2,128,128]{3,2,1,0:T(8,128)} copy(f32[3,2,128,128]{3,2,1,0:T(8,128)} %correct.1) | data formatting | bytes 786432
